TPU v7x, 32 devices: a whole 2x2x4 slice. The times are simulated.
32 devices in a mesh: phi: 4 (over y, x), theta: 8 (over z, core).
Axes of the slice: x: 2, y: 2, z: 4, core: 2. Of those that a mesh axis runs over, the one named last changes fastest.
Arguments:
- subtree_pattern: bfloat16 [256, 2, 32, 64, 128], P(('phi', 'theta')), may hold values from -6 to 6
- up_phi: bfloat16 [128, 256], replicated, may hold values from -0.5 to 0.5
- up_theta: bfloat16 [128, 64], replicated, may hold values from -0.75 to 0.75
- offsets: float32 [3, 256], P(None, ('phi', 'theta')), may hold values from -8 to 8
- theta_start: int32 [256], P('theta'), may hold values from -2 to 126, as said below
- theta_frac: float32 [256], P('theta'), may hold values from 0 to 1
- phi_start: int32 [1024], P('phi'), may hold values from -2 to 254, as said below
- phi_frac: float32 [1024], P('phi'), may hold values from 0 to 1
Outputs:
- rcs: float32 [16, 256, 1024], P(None, 'theta', 'phi')
Inputs may be any that keep to these rules, and one draw needn't show every extreme that they name: `theta_start`: row o lies in polar band b = o // 32; its start is b * (128 // 8) + k with k from -2 to 128 // 8 - 2; the first row of each band has k = -2 and the last k = 128 // 8 - 2. `phi_start`: column w lies in azimuth band b = w // 256; its start is b * (256 // 4) + k with k from -2 to 256 // 4 - 2, read periodically; the first column of each band has k = -2 and the last k = 256 // 4 - 2.
All inputs are finite; a program needn't handle non-finite values.
Results may differ from a plain program's by a relative error of at most 0.0024.
Values sent between devices are 32-bit elements; how exact they have to be, the bound alone decides.
A program may use at most 128 MiB of HBM per device.

v0:
```python
import math

import jax
import jax.numpy as jnp
from jax import lax
from jax.sharding import PartitionSpec as P

NT = 128
NP = 256


def padded_2(block, sides, width, periodic):
    for axis, dim in sides:
        count = lax.axis_size(axis)
        forward = [(i, i + 1) for i in range(count - 1)]
        if periodic:
            forward.append((count - 1, 0))
        backward = [(target, source) for source, target in forward]
        low = lax.ppermute(
            lax.slice_in_dim(block, block.shape[dim] - width, None, axis=dim), axis, forward
        )
        high = lax.ppermute(lax.slice_in_dim(block, 0, width, axis=dim), axis, backward)
        block = jnp.concatenate([low, block, high], axis=dim)
    return block


def directions():
    polar = (jnp.arange(NT, dtype=jnp.float32) + 0.5) * (math.pi / NT)
    azimuth = jnp.arange(NP, dtype=jnp.float32) * (2.0 * math.pi / NP)
    sine_polar = jnp.sin(polar)[:, None]
    unit_x = sine_polar * jnp.cos(azimuth)[None, :]
    unit_y = sine_polar * jnp.sin(azimuth)[None, :]
    unit_z = jnp.cos(polar)[:, None] * jnp.ones((1, NP), jnp.float32)
    return (unit_x, unit_y, unit_z)


def shift_centre(fine_grid, offset, unit_x, unit_y, unit_z):
    phase_angle = 2.0 * math.pi * (offset[0] * unit_x + offset[1] * unit_y + offset[2] * unit_z)
    cosine = jnp.cos(phase_angle)
    sine_part = jnp.sin(phase_angle)
    real_part = fine_grid[0] * cosine - fine_grid[1] * sine_part
    imag_part = fine_grid[0] * sine_part + fine_grid[1] * cosine
    return jnp.stack([real_part, imag_part])


def lagrange_matrix(start, frac, width):
    position = 1.0 + frac
    weights = [
        -(position - 1.0) * (position - 2.0) * (position - 3.0) / 6.0,
        position * (position - 2.0) * (position - 3.0) / 2.0,
        -position * (position - 1.0) * (position - 3.0) / 2.0,
        position * (position - 1.0) * (position - 2.0) / 6.0,
    ]
    columns = jnp.arange(width, dtype=jnp.int32)[None, :]
    matrix = jnp.zeros((start.shape[0], width), jnp.float32)
    for tap in range(4):
        matrix = matrix + jnp.where(columns == (start + tap)[:, None], weights[tap][:, None], 0.0)
    return matrix


def per_device(
    subtree_pattern, up_phi, up_theta, offsets, theta_start, theta_frac, phi_start, phi_frac
):
    unit_x, unit_y, unit_z = directions()
    channels = subtree_pattern.shape[2]

    def add_subtree(total, inputs):
        pattern, offset = inputs
        coarse = jnp.einsum(
            "rqmp,pn->rqmn", pattern, up_phi, preferred_element_type=jnp.float32
        ).astype(jnp.bfloat16)
        fine_grid = jnp.einsum(
            "tm,rqmn->rqtn", up_theta, coarse, preferred_element_type=jnp.float32
        )
        return (total + shift_centre(fine_grid, offset, unit_x, unit_y, unit_z), None)

    zeros = jnp.zeros((2, channels, NT, NP), jnp.float32)
    total, ignored = lax.scan(add_subtree, zeros, (subtree_pattern, offsets.T))
    count_phi = lax.axis_size("phi")
    count_theta = lax.axis_size("theta")
    band_theta = NT // count_theta
    band_phi = NP // count_phi
    partial_band = lax.psum_scatter(total, "theta", scatter_dimension=2, tiled=True)
    root = lax.psum_scatter(partial_band, "phi", scatter_dimension=3, tiled=True)
    padded = padded_2(root, (("theta", 2),), 2, False)
    padded = padded_2(padded, (("phi", 3),), 2, True)
    local_theta = theta_start - lax.axis_index("theta") * band_theta + 2
    local_phi = phi_start - lax.axis_index("phi") * band_phi + 2
    theta_weights = lagrange_matrix(local_theta, theta_frac, band_theta + 4)
    phi_weights = lagrange_matrix(local_phi, phi_frac, band_phi + 4)
    field = jnp.einsum("ot,rqtp->rqop", theta_weights, padded, precision=lax.Precision.HIGHEST)
    field = jnp.einsum("rqop,wp->rqow", field, phi_weights, precision=lax.Precision.HIGHEST)
    subtrees = subtree_pattern.shape[0] * count_phi * count_theta
    power = (field * field).reshape(4, channels // 2, field.shape[2], field.shape[3])
    return jnp.sum(power, axis=0) / subtrees


def solution(mesh):
    return jax.shard_map(
        per_device,
        mesh=mesh,
        in_specs=(
            P(("phi", "theta"), None, None, None, None),
            P(),
            P(),
            P(None, ("phi", "theta")),
            P("theta"),
            P("theta"),
            P("phi"),
            P("phi"),
        ),
        out_specs=P(None, "theta", "phi"),
        check_vma=False,
    )
```

profile of v0, /device:TPU:1, one launch (start us, length us, event | category | flops | bytes accessed | tf_op | source)
XLA Modules:
  0.0 408.6 jit_solution(6019097908202354479)
XLA Ops:
  6.6 231.3 %while.13 = (s32[]{:T(128)}, f32[2,32,128,256]{2,3,1,0:T(8,128)}, bf16[8,2,32,64,128]{4,3,2,1,0:T(8,128)(2,1)}, bf16[128,256]{1,0:T(8,128)(2,1)}, bf16[128,64]{0...) while((s32[]{:T(128)}, f32[2,32,128,256]{2,3,1,0:T(8,128)}, ...), condition=%wide.region_1.2_spmd.clone.clone.clone, body=%wide.region_0.1_spmd.clone.clone.clone.sunk | while | flops 550731904 | bytes 51991228 | solution.py:78
  17.6 8.4 %multiply_subtract_fusion.2 = (f32[1,32,128,256]{2,3,1,0:T(8,128)}, f32[1,32,128,256]{2,3,1,0:T(8,128)}) fusion(f32[2,32,128,256]{2,3,1,0:T(8,128)} %convolution_bitcast_fusion.3, f32[128,256]{0,1:T(8,128)S(1)} %get-tuple-element.275, f32[128,256]{0,1:T(8,128)S(1)} %get-tuple-element.276), kind=kLoop, calls=%fused_computation.5.clone.1 | loop fusion | flops 6291456 | bytes 17039360 | tf_op jit(solution)/shard_map/while/body/eval_jaxpr/sub | solution.py:41
  43.2 8.4 %multiply_subtract_fusion.2 = (f32[1,32,128,256]{2,3,1,0:T(8,128)}, f32[1,32,128,256]{2,3,1,0:T(8,128)}) fusion(f32[2,32,128,256]{2,3,1,0:T(8,128)} %convolution_bitcast_fusion.3, f32[128,256]{0,1:T(8,128)S(1)} %get-tuple-element.275, f32[128,256]{0,1:T(8,128)S(1)} %get-tuple-element.276), kind=kLoop, calls=%fused_computation.5.clone.1 | loop fusion | flops 6291456 | bytes 17039360 | tf_op jit(solution)/shard_map/while/body/eval_jaxpr/sub | solution.py:41
  51.6 10.0 %maximum_add_fusion.2 = f32[2,32,128,256]{2,3,1,0:T(8,128)} fusion(f32[1,32,128,256]{2,3,1,0:T(8,128)} %get-tuple-element.277, f32[1,32,128,256]{2,3,1,0:T(8,128)} %get-tuple-element.278, f32[2,32,128,256]{2,3,1,0:T(8,128)} %get-tuple-element.292, pred[]{:T(512)S(6)} %compare.5), kind=kLoop, calls=%fused_computation.3.clone.1 | loop fusion | flops 6291456 | bytes 25165824 | tf_op jit(solution)/shard_map/while/body/eval_jaxpr/add | solution.py:75
  72.6 8.4 %multiply_subtract_fusion.2 = (f32[1,32,128,256]{2,3,1,0:T(8,128)}, f32[1,32,128,256]{2,3,1,0:T(8,128)}) fusion(f32[2,32,128,256]{2,3,1,0:T(8,128)} %convolution_bitcast_fusion.3, f32[128,256]{0,1:T(8,128)S(1)} %get-tuple-element.275, f32[128,256]{0,1:T(8,128)S(1)} %get-tuple-element.276), kind=kLoop, calls=%fused_computation.5.clone.1 | loop fusion | flops 6291456 | bytes 17039360 | tf_op jit(solution)/shard_map/while/body/eval_jaxpr/sub | solution.py:41
  81.0 10.0 %maximum_add_fusion.2 = f32[2,32,128,256]{2,3,1,0:T(8,128)} fusion(f32[1,32,128,256]{2,3,1,0:T(8,128)} %get-tuple-element.277, f32[1,32,128,256]{2,3,1,0:T(8,128)} %get-tuple-element.278, f32[2,32,128,256]{2,3,1,0:T(8,128)} %get-tuple-element.292, pred[]{:T(512)S(6)} %compare.5), kind=kLoop, calls=%fused_computation.3.clone.1 | loop fusion | flops 6291456 | bytes 25165824 | tf_op jit(solution)/shard_map/while/body/eval_jaxpr/add | solution.py:75
  94.9 7.0 %convolution_bitcast_fusion.3 = f32[2,32,128,256]{2,3,1,0:T(8,128)} fusion(bf16[8,2,32,64,128]{4,3,2,1,0:T(8,128)(2,1)} %get-tuple-element.305, s32[]{:T(128)} %get-tuple-element.291, bf16[128,256]{1,0:T(8,128)(2,1)} %get-tuple-element.306, bf16[128,64]{0,1:T(8,128)(2,1)} %get-tuple-element.307), kind=kOutput, calls=%fused_computation.6.clone.1 | convolution fusion | flops 537919488 | bytes 9519616 | tf_op jit(solution)/shard_map/while/body/eval_jaxpr/tm,rqmn->rqtn/dot_general | solution.py:72
  102.0 8.4 %multiply_subtract_fusion.2 = (f32[1,32,128,256]{2,3,1,0:T(8,128)}, f32[1,32,128,256]{2,3,1,0:T(8,128)}) fusion(f32[2,32,128,256]{2,3,1,0:T(8,128)} %convolution_bitcast_fusion.3, f32[128,256]{0,1:T(8,128)S(1)} %get-tuple-element.275, f32[128,256]{0,1:T(8,128)S(1)} %get-tuple-element.276), kind=kLoop, calls=%fused_computation.5.clone.1 | loop fusion | flops 6291456 | bytes 17039360 | tf_op jit(solution)/shard_map/while/body/eval_jaxpr/sub | solution.py:41
  110.4 10.0 %maximum_add_fusion.2 = f32[2,32,128,256]{2,3,1,0:T(8,128)} fusion(f32[1,32,128,256]{2,3,1,0:T(8,128)} %get-tuple-element.277, f32[1,32,128,256]{2,3,1,0:T(8,128)} %get-tuple-element.278, f32[2,32,128,256]{2,3,1,0:T(8,128)} %get-tuple-element.292, pred[]{:T(512)S(6)} %compare.5), kind=kLoop, calls=%fused_computation.3.clone.1 | loop fusion | flops 6291456 | bytes 25165824 | tf_op jit(solution)/shard_map/while/body/eval_jaxpr/add | solution.py:75
  124.3 7.0 %convolution_bitcast_fusion.3 = f32[2,32,128,256]{2,3,1,0:T(8,128)} fusion(bf16[8,2,32,64,128]{4,3,2,1,0:T(8,128)(2,1)} %get-tuple-element.305, s32[]{:T(128)} %get-tuple-element.291, bf16[128,256]{1,0:T(8,128)(2,1)} %get-tuple-element.306, bf16[128,64]{0,1:T(8,128)(2,1)} %get-tuple-element.307), kind=kOutput, calls=%fused_computation.6.clone.1 | convolution fusion | flops 537919488 | bytes 9519616 | tf_op jit(solution)/shard_map/while/body/eval_jaxpr/tm,rqmn->rqtn/dot_general | solution.py:72
  131.4 8.4 %multiply_subtract_fusion.2 = (f32[1,32,128,256]{2,3,1,0:T(8,128)}, f32[1,32,128,256]{2,3,1,0:T(8,128)}) fusion(f32[2,32,128,256]{2,3,1,0:T(8,128)} %convolution_bitcast_fusion.3, f32[128,256]{0,1:T(8,128)S(1)} %get-tuple-element.275, f32[128,256]{0,1:T(8,128)S(1)} %get-tuple-element.276), kind=kLoop, calls=%fused_computation.5.clone.1 | loop fusion | flops 6291456 | bytes 17039360 | tf_op jit(solution)/shard_map/while/body/eval_jaxpr/sub | solution.py:41
  139.8 10.0 %maximum_add_fusion.2 = f32[2,32,128,256]{2,3,1,0:T(8,128)} fusion(f32[1,32,128,256]{2,3,1,0:T(8,128)} %get-tuple-element.277, f32[1,32,128,256]{2,3,1,0:T(8,128)} %get-tuple-element.278, f32[2,32,128,256]{2,3,1,0:T(8,128)} %get-tuple-element.292, pred[]{:T(512)S(6)} %compare.5), kind=kLoop, calls=%fused_computation.3.clone.1 | loop fusion | flops 6291456 | bytes 25165824 | tf_op jit(solution)/shard_map/while/body/eval_jaxpr/add | solution.py:75
  153.7 7.0 %convolution_bitcast_fusion.3 = f32[2,32,128,256]{2,3,1,0:T(8,128)} fusion(bf16[8,2,32,64,128]{4,3,2,1,0:T(8,128)(2,1)} %get-tuple-element.305, s32[]{:T(128)} %get-tuple-element.291, bf16[128,256]{1,0:T(8,128)(2,1)} %get-tuple-element.306, bf16[128,64]{0,1:T(8,128)(2,1)} %get-tuple-element.307), kind=kOutput, calls=%fused_computation.6.clone.1 | convolution fusion | flops 537919488 | bytes 9519616 | tf_op jit(solution)/shard_map/while/body/eval_jaxpr/tm,rqmn->rqtn/dot_general | solution.py:72
  160.8 8.4 %multiply_subtract_fusion.2 = (f32[1,32,128,256]{2,3,1,0:T(8,128)}, f32[1,32,128,256]{2,3,1,0:T(8,128)}) fusion(f32[2,32,128,256]{2,3,1,0:T(8,128)} %convolution_bitcast_fusion.3, f32[128,256]{0,1:T(8,128)S(1)} %get-tuple-element.275, f32[128,256]{0,1:T(8,128)S(1)} %get-tuple-element.276), kind=kLoop, calls=%fused_computation.5.clone.1 | loop fusion | flops 6291456 | bytes 17039360 | tf_op jit(solution)/shard_map/while/body/eval_jaxpr/sub | solution.py:41
  169.2 10.0 %maximum_add_fusion.2 = f32[2,32,128,256]{2,3,1,0:T(8,128)} fusion(f32[1,32,128,256]{2,3,1,0:T(8,128)} %get-tuple-element.277, f32[1,32,128,256]{2,3,1,0:T(8,128)} %get-tuple-element.278, f32[2,32,128,256]{2,3,1,0:T(8,128)} %get-tuple-element.292, pred[]{:T(512)S(6)} %compare.5), kind=kLoop, calls=%fused_computation.3.clone.1 | loop fusion | flops 6291456 | bytes 25165824 | tf_op jit(solution)/shard_map/while/body/eval_jaxpr/add | solution.py:75
  183.1 7.0 %convolution_bitcast_fusion.3 = f32[2,32,128,256]{2,3,1,0:T(8,128)} fusion(bf16[8,2,32,64,128]{4,3,2,1,0:T(8,128)(2,1)} %get-tuple-element.305, s32[]{:T(128)} %get-tuple-element.291, bf16[128,256]{1,0:T(8,128)(2,1)} %get-tuple-element.306, bf16[128,64]{0,1:T(8,128)(2,1)} %get-tuple-element.307), kind=kOutput, calls=%fused_computation.6.clone.1 | convolution fusion | flops 537919488 | bytes 9519616 | tf_op jit(solution)/shard_map/while/body/eval_jaxpr/tm,rqmn->rqtn/dot_general | solution.py:72
  190.1 8.4 %multiply_subtract_fusion.2 = (f32[1,32,128,256]{2,3,1,0:T(8,128)}, f32[1,32,128,256]{2,3,1,0:T(8,128)}) fusion(f32[2,32,128,256]{2,3,1,0:T(8,128)} %convolution_bitcast_fusion.3, f32[128,256]{0,1:T(8,128)S(1)} %get-tuple-element.275, f32[128,256]{0,1:T(8,128)S(1)} %get-tuple-element.276), kind=kLoop, calls=%fused_computation.5.clone.1 | loop fusion | flops 6291456 | bytes 17039360 | tf_op jit(solution)/shard_map/while/body/eval_jaxpr/sub | solution.py:41
  198.6 10.0 %maximum_add_fusion.2 = f32[2,32,128,256]{2,3,1,0:T(8,128)} fusion(f32[1,32,128,256]{2,3,1,0:T(8,128)} %get-tuple-element.277, f32[1,32,128,256]{2,3,1,0:T(8,128)} %get-tuple-element.278, f32[2,32,128,256]{2,3,1,0:T(8,128)} %get-tuple-element.292, pred[]{:T(512)S(6)} %compare.5), kind=kLoop, calls=%fused_computation.3.clone.1 | loop fusion | flops 6291456 | bytes 25165824 | tf_op jit(solution)/shard_map/while/body/eval_jaxpr/add | solution.py:75
  212.5 7.0 %convolution_bitcast_fusion.3 = f32[2,32,128,256]{2,3,1,0:T(8,128)} fusion(bf16[8,2,32,64,128]{4,3,2,1,0:T(8,128)(2,1)} %get-tuple-element.305, s32[]{:T(128)} %get-tuple-element.291, bf16[128,256]{1,0:T(8,128)(2,1)} %get-tuple-element.306, bf16[128,64]{0,1:T(8,128)(2,1)} %get-tuple-element.307), kind=kOutput, calls=%fused_computation.6.clone.1 | convolution fusion | flops 537919488 | bytes 9519616 | tf_op jit(solution)/shard_map/while/body/eval_jaxpr/tm,rqmn->rqtn/dot_general | solution.py:72
  219.5 8.4 %multiply_subtract_fusion.2 = (f32[1,32,128,256]{2,3,1,0:T(8,128)}, f32[1,32,128,256]{2,3,1,0:T(8,128)}) fusion(f32[2,32,128,256]{2,3,1,0:T(8,128)} %convolution_bitcast_fusion.3, f32[128,256]{0,1:T(8,128)S(1)} %get-tuple-element.275, f32[128,256]{0,1:T(8,128)S(1)} %get-tuple-element.276), kind=kLoop, calls=%fused_computation.5.clone.1 | loop fusion | flops 6291456 | bytes 17039360 | tf_op jit(solution)/shard_map/while/body/eval_jaxpr/sub | solution.py:41
  228.0 10.0 %maximum_add_fusion.2 = f32[2,32,128,256]{2,3,1,0:T(8,128)} fusion(f32[1,32,128,256]{2,3,1,0:T(8,128)} %get-tuple-element.277, f32[1,32,128,256]{2,3,1,0:T(8,128)} %get-tuple-element.278, f32[2,32,128,256]{2,3,1,0:T(8,128)} %get-tuple-element.292, pred[]{:T(512)S(6)} %compare.5), kind=kLoop, calls=%fused_computation.3.clone.1 | loop fusion | flops 6291456 | bytes 25165824 | tf_op jit(solution)/shard_map/while/body/eval_jaxpr/add | solution.py:75
  238.0 10.3 %copy.22 = f32[2,32,128,256]{3,1,0,2:T(8,128)} copy(f32[2,32,128,256]{2,3,1,0:T(8,128)} %get-tuple-element.52) | data formatting | bytes 16777216 | tf_op jit(solution)/shard_map/while | solution.py:78
  248.3 89.8 %reduce-scatter.5.cloned.1.call-done = f32[2,32,16,256]{3,1,0,2:T(8,128)} async-done(((f32[2,32,128,256]{3,1,0,2:T(8,128)}), f32[2,32,16,256]{3,1,0,2:T(8,128)}) %reduce-scatter.5.cloned.1.call-update) | async-done | bytes 1048592 | tf_op jit(solution)/shard_map/reduce_scatter | solution.py:83
  351.7 28.2 %reduce-scatter.7.cloned.1.call-done = f32[64,1024]{1,0:T(8,128)} async-done(((f32[256,1024]{1,0:T(8,128)}), f32[64,1024]{1,0:T(8,128)}) %reduce-scatter.7.cloned.1.call-update) | async-done | bytes 262160
  (83 shorter events, 93.8 us)
Async XLA Ops:
  6.5 331.6 %reduce-scatter.5.cloned.1.call-start = ((), (), s32[]{:S(2)}) async-start(), calls=%async_computation.2 | async-start | bytes 9437184 | tf_op jit(solution)/shard_map/reduce_scatter | solution.py:83
  248.3 131.7 %reduce-scatter.7.cloned.1.call-start = ((), (), s32[]{:S(2)}) async-start(), calls=%async_computation.3 | async-start | bytes 1310720
  344.6 7.0 %copy-start.2 = (f32[32]{0:T(128)S(1)}, f32[32]{0:T(128)}, u32[]{:S(2)}) copy-start(f32[32]{0:T(128)} %param.15) | copy-start | bytes 388
  344.6 7.1 %copy-start = (f32[256]{0:T(256)S(1)}, f32[256]{0:T(256)}, u32[]{:S(2)}) copy-start(f32[256]{0:T(256)} %param.17) | copy-start | bytes 3076
  344.6 7.1 %copy-start.1 = (s32[256]{0:T(256)S(1)}, s32[256]{0:T(256)}, u32[]{:S(2)}) copy-start(s32[256]{0:T(256)} %param.16) | copy-start | bytes 3076
  344.6 43.2 %copy-start.3 = (s32[32]{0:T(128)S(1)}, s32[32]{0:T(128)}, u32[]{:S(2)}) copy-start(s32[32]{0:T(128)} %param.14) | copy-start | bytes 388
  381.9 6.5 %collective-permute-start = (f32[2,32,2,64]{3,1,2,0:T(8,128)S(1)}, f32[2,32,2,64]{3,1,2,0:T(8,128)S(1)}, u32[]{:S(2)}, u32[]{:S(2)}) collective-permute-start(f32[2,32,2,64]{3,1,2,0:T(8,128)S(1)} %copy.23), channel_id=1, source_target_pairs={{0,1},{1,2},{2,3},{3,4},{4,5},{5,6},{6,7},{8,9},{9,10},{10,11},{11... | collective-permute-start | bytes 98312 | tf_op jit(solution)/shard_map/ppermute | solution.py:19
  385.8 5.6 %collective-permute-start.1 = (f32[2,32,2,64]{3,1,2,0:T(8,128)S(1)}, f32[2,32,2,64]{3,1,2,0:T(8,128)S(1)}, u32[]{:S(2)}, u32[]{:S(2)}) collective-permute-start(f32[2,32,2,64]{3,1,2,0:T(8,128)S(1)} %copy.24), channel_id=1, source_target_pairs={{1,0},{2,1},{3,2},{4,3},{5,4},{6,5},{7,6},{9,8},{10,9},{11,10},{12... | collective-permute-start | bytes 98312 | tf_op jit(solution)/shard_map/ppermute | solution.py:22
  392.2 3.8 collective-permute-start.2
  393.8 3.1 collective-permute-start.3
Sparse Core Ops, SparseCore 0:
  248.4 89.7 reduce-scatter.4
  351.8 28.1 reduce-scatter.6
where the time goes:
time: 410 us; the launch traced here: 409 us
  other arithmetic  165 us (40%)
  waiting for transfers between devices  122 us (30%)
  matrix products  59.8 us (15%)
  local copies, waits for them, and re-layouts  39 us (10%)
  between operations  13.6 us (3%)
  starting transfers between devices  8.42 us (2%)
    reduce_scatter x1, waiting for transfers between devices, per_device(): lax.psum_scatter(total, 'theta', scatter_dimension=2, tiled=True)  89.8 us
    add x8, other arithmetic, add_subtree(): total + shift_centre(fine_grid, offset, unit_x, unit_y, unit_z)  76.5 us
    sub x8, other arithmetic, shift_centre(): real_part = fine_grid[0] * cosine - fine_grid[1] * sine_part  67.3 us
    dot_general x8, matrix products, add_subtree(): jnp.einsum('tm,rqmn->rqtn', up_theta, coarse, preferred_element_type=jnp....  56.4 us
    unnamed x3, waiting for transfers between devices  28.2 us
    unnamed x11, local copies, waits for them, and re-layouts  15.3 us
    cos x8, other arithmetic, shift_centre(): cosine = jnp.cos(phase_angle)  14.7 us
    while x1, local copies, waits for them, and re-layouts, per_device(): total, ignored = lax.scan(add_subtree, zeros, (subtree_pattern, offsets.T))  10.3 us
  transfers between devices with their start and end apart: 6, of which 5 were waited for; matrix products, arithmetic and copies ran while one was open for 0% of the time, Pallas kernels for 0%

commit v1 on v0

v1 whole, which is shorter than its diff:
```python
import functools
import math

import jax
import jax.numpy as jnp
import numpy as np
from jax import lax
from jax.experimental import pallas as pl
from jax.experimental.pallas import tpu as pltpu
from jax.sharding import PartitionSpec as P

NT = 128
NP = 256
LANES = 128


def padded_2(block, sides, width, periodic):
    for axis, dim in sides:
        count = lax.axis_size(axis)
        forward = [(i, i + 1) for i in range(count - 1)]
        if periodic:
            forward.append((count - 1, 0))
        backward = [(target, source) for source, target in forward]
        low = lax.ppermute(
            lax.slice_in_dim(block, block.shape[dim] - width, None, axis=dim), axis, forward
        )
        high = lax.ppermute(lax.slice_in_dim(block, 0, width, axis=dim), axis, backward)
        block = jnp.concatenate([low, block, high], axis=dim)
    return block


def direction_tables(group, bands):
    polar = (np.arange(NT) + 0.5) * (math.pi / NT)
    rows = np.stack([np.sin(polar), np.cos(polar)])[:, :, None]
    rows = np.broadcast_to(rows, (2, NT, LANES))
    azimuth = (np.arange(NP) * (2.0 * math.pi / NP)).reshape(bands, 1, -1)
    azimuth = np.broadcast_to(azimuth, (bands, group, azimuth.shape[2])).reshape(1, -1)
    columns = np.stack([np.cos(azimuth), np.sin(azimuth)])
    columns = np.broadcast_to(columns, (2, 8, columns.shape[2]))
    return rows.astype(np.float32), columns.astype(np.float32)


def grouped_up_phi(up_phi, group, bands):
    split = up_phi.reshape(up_phi.shape[0], bands, 1, NP // bands)
    blocks = []
    for g in range(group):
        pads = [(0, 0), (0, 0), (g, group - 1 - g), (0, 0)]
        blocks.append(jnp.pad(split, pads).reshape(up_phi.shape[0], -1))
    return jnp.concatenate(blocks, axis=0)


def turn_series():
    two_pi = 2.0 * math.pi
    sine = [(-1) ** k * two_pi ** (2 * k + 1) / math.factorial(2 * k + 1) for k in range(9)]
    cosine = [(-1) ** k * two_pi ** (2 * k) / math.factorial(2 * k) for k in range(10)]
    return sine, cosine


def horner(square, terms):
    value = jnp.full_like(square, terms[-1])
    for term in terms[-2::-1]:
        value = value * square + term
    return value


def phase_factors(offsets_ref, row_ref, column_ref, cos_ref, sin_ref):
    sine_terms, cosine_terms = turn_series()
    lane_groups = cos_ref.shape[2] // LANES

    @pl.loop(0, cos_ref.shape[0])
    def _(s):
        off_x, off_y, off_z = (offsets_ref[k, s] for k in range(3))
        for lane in range(lane_groups):
            lanes = slice(lane * LANES, (lane + 1) * LANES)
            wave = off_x * column_ref[0, 0:1, lanes] + off_y * column_ref[1, 0:1, lanes]
            turns = wave * row_ref[0] + off_z * row_ref[1]
            turns = turns - jnp.floor(turns + 0.5)
            square = turns * turns
            cos_ref[s, :, lanes] = horner(square, cosine_terms)
            sin_ref[s, :, lanes] = horner(square, sine_terms) * turns


def subtree_sum(i, pattern_ref, phi_ref, theta_ref, coarse_ref, cos_ref, sin_ref, store):
    count, parts, group, _, polar, _ = pattern_ref.shape
    rows = [
        jnp.concatenate([pattern_ref[s, r, g, i] for g in range(group)], axis=1)
        for s in range(count)
        for r in range(parts)
    ]
    coarse_ref[...] = jnp.dot(
        jnp.concatenate(rows, axis=0), phi_ref[...], preferred_element_type=jnp.float32
    ).astype(jnp.bfloat16)
    width = 2 * LANES
    for start in range(0, phi_ref.shape[1], width):
        lanes = slice(start, start + width)
        real_sum, imag_sum = None, None
        for s in range(count):
            real, imag = (
                jnp.dot(
                    theta_ref[...],
                    coarse_ref[(s * parts + r) * polar : (s * parts + r + 1) * polar, lanes],
                    preferred_element_type=jnp.float32,
                )
                for r in range(parts)
            )
            cosine, sine = cos_ref[s, :, lanes], sin_ref[s, :, lanes]
            real_part = real * cosine - imag * sine
            imag_part = real * sine + imag * cosine
            real_sum = real_part if s == 0 else real_sum + real_part
            imag_sum = imag_part if s == 0 else imag_sum + imag_part
        for k in range(width // LANES):
            piece = slice(k * LANES, (k + 1) * LANES)
            store(start // LANES + k, 0, real_sum[:, piece])
            store(start // LANES + k, 1, imag_sum[:, piece])


def sum_kernel(
    pattern_ref, phi_ref, theta_ref, offsets_ref, row_ref, column_ref, out_ref,
    cos_ref, sin_ref, coarse_ref,
):
    phase_factors(offsets_ref, row_ref, column_ref, cos_ref, sin_ref)
    bands_theta, _, _, units, band_theta, _ = out_ref.shape

    @pl.loop(0, units)
    def _(i):
        def store(band, part, value):
            out_ref[:, band, part, i] = value.reshape(bands_theta, band_theta, LANES)

        subtree_sum(i, pattern_ref, phi_ref, theta_ref, coarse_ref, cos_ref, sin_ref, store)


def lagrange_matrix(start, frac, width):
    position = 1.0 + frac
    weights = [
        -(position - 1.0) * (position - 2.0) * (position - 3.0) / 6.0,
        position * (position - 2.0) * (position - 3.0) / 2.0,
        -position * (position - 1.0) * (position - 3.0) / 2.0,
        position * (position - 1.0) * (position - 2.0) / 6.0,
    ]
    columns = jnp.arange(width, dtype=jnp.int32)[None, :]
    matrix = jnp.zeros((start.shape[0], width), jnp.float32)
    for tap in range(4):
        matrix = matrix + jnp.where(columns == (start + tap)[:, None], weights[tap][:, None], 0.0)
    return matrix


def per_device(
    subtree_pattern, up_phi, up_theta, offsets, theta_start, theta_frac, phi_start, phi_frac
):
    count_phi = lax.axis_size("phi")
    count_theta = lax.axis_size("theta")
    band_theta = NT // count_theta
    band_phi = NP // count_phi
    group = LANES // band_phi
    held, parts, channels, polar, azimuth = subtree_pattern.shape
    units = channels // group
    pattern = subtree_pattern.reshape(held, parts, group, units, polar, azimuth)
    up_phi_grouped = grouped_up_phi(up_phi, group, count_phi)
    rows, columns = direction_tables(group, count_phi)
    whole = pl.BlockSpec(memory_space=pltpu.VMEM)
    total = pl.pallas_call(
        sum_kernel,
        out_shape=jax.ShapeDtypeStruct(
            (count_theta, count_phi, parts, units, band_theta, LANES), jnp.float32
        ),
        in_specs=[whole, whole, whole, pl.BlockSpec(memory_space=pltpu.SMEM), whole, whole],
        out_specs=whole,
        scratch_shapes=[
            pltpu.VMEM((held, NT, count_phi * LANES), jnp.float32),
            pltpu.VMEM((held, NT, count_phi * LANES), jnp.float32),
            pltpu.VMEM((held * parts * polar, count_phi * LANES), jnp.bfloat16),
        ],
        compiler_params=pltpu.CompilerParams(vmem_limit_bytes=56 << 20),
    )(pattern, up_phi_grouped, up_theta, offsets, jnp.asarray(rows), jnp.asarray(columns))
    partial_band = lax.psum_scatter(total, "theta", scatter_dimension=0, tiled=False)
    root = lax.psum_scatter(partial_band, "phi", scatter_dimension=0, tiled=False)
    root = root.reshape(parts, units, band_theta, group, band_phi)
    root = root.transpose(0, 3, 1, 2, 4).reshape(parts, channels, band_theta, band_phi)
    padded = padded_2(root, (("theta", 2),), 2, False)
    padded = padded_2(padded, (("phi", 3),), 2, True)
    local_theta = theta_start - lax.axis_index("theta") * band_theta + 2
    local_phi = phi_start - lax.axis_index("phi") * band_phi + 2
    theta_weights = lagrange_matrix(local_theta, theta_frac, band_theta + 4)
    phi_weights = lagrange_matrix(local_phi, phi_frac, band_phi + 4)
    field = jnp.einsum("ot,rqtp->rqop", theta_weights, padded, precision=lax.Precision.HIGHEST)
    field = jnp.einsum("rqop,wp->rqow", field, phi_weights, precision=lax.Precision.HIGHEST)
    subtrees = held * count_phi * count_theta
    power = (field * field).reshape(4, channels // 2, field.shape[2], field.shape[3])
    return jnp.sum(power, axis=0) / subtrees


def solution(mesh):
    return jax.shard_map(
        per_device,
        mesh=mesh,
        in_specs=(
            P(("phi", "theta"), None, None, None, None),
            P(),
            P(),
            P(None, ("phi", "theta")),
            P("theta"),
            P("theta"),
            P("phi"),
            P("phi"),
        ),
        out_specs=P(None, "theta", "phi"),
        check_vma=False,
    )
```

time: 410 us -> 186 us (0.45)
  other arithmetic: 165 us -> 1.93 us
  matrix products: 59.8 us -> 3.44 us
  local copies, waits for them, and re-layouts: 39 us -> 5.67 us
  Pallas kernels: 0 us -> 26.9 us
    add x8 -> x0, other arithmetic: 76.5 us -> none  [add_subtree(): total + shift_centre(fine_grid, offset, unit_x, unit_y, unit_z)]
    sub x8 -> x0, other arithmetic: 67.3 us -> none  [shift_centre(): real_part = fine_grid[0] * cosine - fine_grid[1] * sine_part]
    dot_general x8 -> x0, matrix products: 56.4 us -> none  [add_subtree(): jnp.einsum('tm,rqmn->rqtn', up_theta, coarse, preferred_element_type=jnp....]
    pallas_call x0 -> x1, Pallas kernels: none -> 26.9 us  [per_device(): pl.pallas_call(sum_kernel, out_shape=jax.ShapeDtypeStruct((count_theta, c...]
    cos x9 -> x0, other arithmetic: 14.8 us -> none  [the longest x8 14.7 us: shift_centre(): cosine = jnp.cos(phase_angle)]
    unnamed x11 -> x10, local copies, waits for them, and re-layouts: 15.3 us -> 2.39 us
    while x1 -> x0, local copies, waits for them, and re-layouts: 10.3 us -> none  [per_device(): total, ignored = lax.scan(add_subtree, zeros, (subtree_pattern, offsets.T))]
    dynamic_slice x8 -> x0, local copies, waits for them, and re-layouts: 6.02 us -> none  [per_device(): total, ignored = lax.scan(add_subtree, zeros, (subtree_pattern, offsets.T))]
where the time goes in v1:
time: 186 us; the launch traced here: 185 us
  waiting for transfers between devices  126 us (68%)
  Pallas kernels  26.9 us (14%)
  between operations  13.6 us (7%)
  starting transfers between devices  8.22 us (4%)
  local copies, waits for them, and re-layouts  5.67 us (3%)
  matrix products  3.44 us (2%)
  other arithmetic  1.93 us (1%)
    reduce_scatter x1, waiting for transfers between devices, per_device(): lax.psum_scatter(total, 'theta', scatter_dimension=0, tiled=False)  89.8 us
    unnamed x3, waiting for transfers between devices  31 us
    pallas_call x1, Pallas kernels, per_device(): pl.pallas_call(sum_kernel, out_shape=jax.ShapeDtypeStruct((count_theta, c...  26.9 us
    ppermute x2, starting transfers between devices, padded_2(): lax.ppermute(lax.slice_in_dim(block, block.shape[dim] - width, None, axis...  5.05 us
    ppermute x2, waiting for transfers between devices, padded_2(): lax.ppermute(lax.slice_in_dim(block, 0, width, axis=dim), axis, backward)  3.9 us
  transfers between devices with their start and end apart: 6, of which 5 were waited for; matrix products, arithmetic and copies ran while one was open for 0% of the time, Pallas kernels for 0%

profile of v1, /device:TPU:1, one launch (start us, length us, event | category | flops | bytes accessed | tf_op | source)
XLA Modules:
  0.0 185.4 jit_solution(11042658524947654321)
XLA Ops:
  6.5 0.9 copy.31
  7.8 1.4 copy.36.theta_ref
  9.2 0.7 pad_maximum_fusion.1.phi_ref
  9.9 26.9 %shard_map.100 = f32[8,4,2,16,16,128]{5,4,3,2,1,0:T(8,128)} custom-call(bf16[8,2,2,16,64,128]{5,4,3,2,1,0:T(8,128)(2,1)} %bitcast.28, bf16[256,512]{1,0:T(8,128)(2,1)} %pad_maximum_fusion.1.phi_ref, bf16[128,64]{1,0:T(8,128)(2,1)} %copy.36.theta_ref, f32[3,8]{1,0:T(4,128)} %offsets_ref.1, f32[2,128,128]{2,1,0:T(8,128)} %constant.73.clone.row_ref, ...), custom_call_target="tpu_custom_call" | custom-call | tf_op jit(solution)/shard_map/pallas_call | solution.py:161
  36.9 89.8 %reduce-scatter.5.cloned.1.call-done = f32[1,4,2,16,16,128]{5,4,3,2,1,0:T(8,128)} async-done(((f32[8,4,2,16,16,128]{5,4,3,2,1,0:T(8,128)}), f32[1,4,2,16,16,128]{5,4,3,2,1,0:T(8,128)}) %reduce-scatter.5.cloned.1.call-update) | async-done | bytes 1048592 | tf_op jit(solution)/shard_map/reduce_scatter | solution.py:175
  126.8 30.9 %reduce-scatter.7.cloned.1.call-done = f32[1,2,16,16,128]{4,3,2,1,0:T(8,128)} async-done(((f32[4,2,16,16,128]{4,3,2,1,0:T(8,128)}), f32[1,2,16,16,128]{4,3,2,1,0:T(8,128)}) %reduce-scatter.7.cloned.1.call-update) | async-done | bytes 262160
  157.7 1.3 reshape_reduce_scatter.3
  159.1 3.8 %collective-permute-start = (f32[2,32,2,64]{3,2,1,0:T(2,128)S(1)}, f32[2,32,2,64]{3,2,1,0:T(2,128)S(1)}, u32[]{:S(2)}, u32[]{:S(2)}) collective-permute-start(f32[2,32,2,64]{3,2,1,0:T(2,128)S(1)} %get-tuple-element.9), channel_id=1, source_target_pairs={{0,1},{1,2},{2,3},{3,4},{4,5},{5,6},{6,7},{8,9},{9,10},{10,11},{11... | collective-permute-start | bytes 98312 | tf_op jit(solution)/shard_map/ppermute | solution.py:24
  162.9 1.9 %collective-permute-start.1 = (f32[2,32,2,64]{3,2,1,0:T(2,128)S(1)}, f32[2,32,2,64]{3,2,1,0:T(2,128)S(1)}, u32[]{:S(2)}, u32[]{:S(2)}) collective-permute-start(f32[2,32,2,64]{3,2,1,0:T(2,128)S(1)} %get-tuple-element.10), channel_id=1, source_target_pairs={{1,0},{2,1},{3,2},{4,3},{5,4},{6,5},{7,6},{9,8},{10,9},{11,10},{12... | collective-permute-start | bytes 98312 | tf_op jit(solution)/shard_map/ppermute | solution.py:27
  164.9 3.6 %collective-permute-done.1 = f32[2,32,2,64]{3,2,1,0:T(2,128)S(1)} collective-permute-done((f32[2,32,2,64]{3,2,1,0:T(2,128)S(1)}, f32[2,32,2,64]{3,2,1,0:T(2,128)S(1)}, u32[]{:S(2)}, u32[]{:S(2)}) %collective-permute-start.1) | collective-permute-done | bytes 32800 | tf_op jit(solution)/shard_map/ppermute | solution.py:27
  168.5 0.1 pad_maximum_fusion
  168.7 0.3 fusion.53
  169.0 0.3 copy.38
  169.3 1.2 collective-permute-start.2
  170.5 0.3 copy.39
  170.8 1.2 collective-permute-start.3
  172.0 1.0 collective-permute-done.2
  173.1 0.4 copy.40
  173.4 0.3 collective-permute-done.3
  173.7 0.4 copy.41
  174.1 1.6 convolution_bitcast_fusion
  175.7 1.8 convolution_multiply_fusion
  177.5 0.2 reduce_sum.9
  177.7 0.8 broadcast_multiply_fusion
  (23 shorter events, 0.5 us)
Async XLA Ops:
  6.5 120.2 %reduce-scatter.5.cloned.1.call-start = ((), (), s32[]{:S(2)}) async-start(), calls=%async_computation.2 | async-start | bytes 9437184 | tf_op jit(solution)/shard_map/reduce_scatter | solution.py:175
  36.8 89.9 %copy-start.2 = (f32[32]{0:T(128)S(1)}, f32[32]{0:T(128)}, u32[]{:S(2)}) copy-start(f32[32]{0:T(128)} %param.15) | copy-start | bytes 388
  36.8 90.0 %copy-start = (f32[256]{0:T(256)S(1)}, f32[256]{0:T(256)}, u32[]{:S(2)}) copy-start(f32[256]{0:T(256)} %param.17) | copy-start | bytes 3076
  36.8 90.0 %copy-start.1 = (s32[256]{0:T(256)S(1)}, s32[256]{0:T(256)}, u32[]{:S(2)}) copy-start(s32[256]{0:T(256)} %param.16) | copy-start | bytes 3076
  36.8 128.1 %copy-start.3 = (s32[32]{0:T(128)S(1)}, s32[32]{0:T(128)}, u32[]{:S(2)}) copy-start(s32[32]{0:T(128)} %param.14) | copy-start | bytes 388
  36.8 120.9 %reduce-scatter.7.cloned.1.call-start = ((), (), s32[]{:S(2)}) async-start(), calls=%async_computation.3 | async-start | bytes 1310720
  159.1 5.8 %collective-permute-start = (f32[2,32,2,64]{3,2,1,0:T(2,128)S(1)}, f32[2,32,2,64]{3,2,1,0:T(2,128)S(1)}, u32[]{:S(2)}, u32[]{:S(2)}) collective-permute-start(f32[2,32,2,64]{3,2,1,0:T(2,128)S(1)} %get-tuple-element.9), channel_id=1, source_target_pairs={{0,1},{1,2},{2,3},{3,4},{4,5},{5,6},{6,7},{8,9},{9,10},{10,11},{11... | collective-permute-start | bytes 98312 | tf_op jit(solution)/shard_map/ppermute | solution.py:24
  162.9 5.6 %collective-permute-start.1 = (f32[2,32,2,64]{3,2,1,0:T(2,128)S(1)}, f32[2,32,2,64]{3,2,1,0:T(2,128)S(1)}, u32[]{:S(2)}, u32[]{:S(2)}) collective-permute-start(f32[2,32,2,64]{3,2,1,0:T(2,128)S(1)} %get-tuple-element.10), channel_id=1, source_target_pairs={{1,0},{2,1},{3,2},{4,3},{5,4},{6,5},{7,6},{9,8},{10,9},{11,10},{12... | collective-permute-start | bytes 98312 | tf_op jit(solution)/shard_map/ppermute | solution.py:27
  169.3 3.8 %collective-permute-start.2 = (f32[2,32,20,2]{1,3,2,0:T(2,128)S(1)}, f32[2,32,20,2]{1,3,2,0:T(2,128)S(1)}, u32[]{:S(2)}, u32[]{:S(2)}) collective-permute-start(f32[2,32,20,2]{1,3,2,0:T(2,128)S(1)} %copy.38), channel_id=1, source_target_pairs={{0,8},{8,16},{16,24},{24,0},{1,9},{9,17},{17,25},{25,1},{2,10},{10... | collective-permute-start | bytes 30728 | tf_op jit(solution)/shard_map/ppermute | solution.py:24
  170.8 2.9 %collective-permute-start.3 = (f32[2,32,20,2]{1,3,2,0:T(2,128)S(1)}, f32[2,32,20,2]{1,3,2,0:T(2,128)S(1)}, u32[]{:S(2)}, u32[]{:S(2)}) collective-permute-start(f32[2,32,20,2]{1,3,2,0:T(2,128)S(1)} %copy.39), channel_id=1, source_target_pairs={{8,0},{16,8},{24,16},{0,24},{9,1},{17,9},{25,17},{1,25},{10,2},{18... | collective-permute-start | bytes 30728 | tf_op jit(solution)/shard_map/ppermute | solution.py:27
Sparse Core Ops, SparseCore 0:
  36.9 89.7 reduce-scatter.4
  129.6 28.1 reduce-scatter.6

commit v2 on v1

--- a/solution.py
+++ b/solution.py
@@ -1,4 +1,3 @@
-import functools
 import math
 
 import jax
@@ -12,6 +11,9 @@
 NT = 128
 NP = 256
 LANES = 128
+CHUNKS = 8
+FIRST_LAG = 3
+SECOND_LAG = 5
 
 
 def padded_2(block, sides, width, periodic):
@@ -80,13 +82,10 @@
             sin_ref[s, :, lanes] = horner(square, sine_terms) * turns
 
 
-def subtree_sum(i, pattern_ref, phi_ref, theta_ref, coarse_ref, cos_ref, sin_ref, store):
-    count, parts, group, _, polar, _ = pattern_ref.shape
-    rows = [
-        jnp.concatenate([pattern_ref[s, r, g, i] for g in range(group)], axis=1)
-        for s in range(count)
-        for r in range(parts)
-    ]
+def subtree_sum(pattern, phi_ref, theta_ref, coarse_ref, cos_ref, sin_ref, store):
+    count, polar = cos_ref.shape[0], theta_ref.shape[1]
+    parts = coarse_ref.shape[0] // (count * polar)
+    rows = [pattern(s, r) for s in range(count) for r in range(parts)]
     coarse_ref[...] = jnp.dot(
         jnp.concatenate(rows, axis=0), phi_ref[...], preferred_element_type=jnp.float32
     ).astype(jnp.bfloat16)
@@ -114,19 +113,228 @@
             store(start // LANES + k, 1, imag_sum[:, piece])
 
 
-def sum_kernel(
-    pattern_ref, phi_ref, theta_ref, offsets_ref, row_ref, column_ref, out_ref,
-    cos_ref, sin_ref, coarse_ref,
+def root_kernel(
+    pattern_hbm, phi_ref, theta_ref, offsets_ref, row_ref, column_ref, out_ref,
+    pattern_ref, cos_ref, sin_ref, coarse_ref, sums,
+    core_in, low_first, high_first, high_second, low_second, far_in,
+    load_sem, core_sem, first_sem, second_sem, far_sem,
 ):
+    chunks, _, n_high, _, n_far, parts, per_chunk, band_theta, _ = sums.shape
+    group = pattern_ref.shape[3]
+    phi, theta = lax.axis_index("phi"), lax.axis_index("theta")
+    high, low = phi // 2, lax.rem(phi, 2)
+    far, core = theta // 2, lax.rem(theta, 2)
+
+    def turned(index, step, count):
+        return lax.rem(index + step, count)
+
+    core_peer = (phi, far * 2 + 1 - core)
+    low_peer = (high * 2 + 1 - low, theta)
+
+    def high_peer(step):
+        return (turned(high, step, n_high) * 2 + low, theta)
+
+    def far_peer(step):
+        return (phi, turned(far, step, n_far) * 2 + core)
+
+    def send(source, target, sems, peer):
+        return pltpu.make_async_remote_copy(
+            src_ref=source,
+            dst_ref=target,
+            send_sem=sems.at[0],
+            recv_sem=sems.at[1],
+            device_id=peer,
+            device_id_type=pl.DeviceIdType.MESH,
+        )
+
+    def core_copies(k):
+        return [send(sums.at[k, 1 - core], core_in.at[k], core_sem.at[k], core_peer)]
+
+    def first_copies(k, parity):
+        if parity == 0:
+            source = sums.at[k, core, :, 1 - low]
+            return [send(source, low_first.at[k // 2], first_sem.at[k, 0], low_peer)]
+        return [
+            send(
+                sums.at[k, core, turned(high, d, n_high)],
+                high_first.at[k // 2, d - 1],
+                first_sem.at[k, d - 1],
+                high_peer(d),
+            )
+            for d in range(1, n_high)
+        ]
+
+    def second_copies(k, parity):
+        if parity == 1:
+            source = sums.at[k, core, high, 1 - low]
+            return [send(source, low_second.at[k // 2], second_sem.at[k, 0], low_peer)]
+        return [
+            send(
+                sums.at[k, core, turned(high, d, n_high), low],
+                high_second.at[k // 2, d - 1],
+                second_sem.at[k, d - 1],
+                high_peer(d),
+            )
+            for d in range(1, n_high)
+        ]
+
+    def far_copies(k):
+        return [
+            send(
+                sums.at[k, core, high, low, turned(far, d, n_far)],
+                far_in.at[k, d - 1],
+                far_sem.at[k, d - 1],
+                far_peer(d),
+            )
+            for d in range(1, n_far)
+        ]
+
+    def start(copies):
+        for copy in copies:
+            copy.start()
+
+    def arrive(copies):
+        for copy in copies:
+            copy.wait_recv()
+
+    def after_core(k, parity):
+        arrive(core_copies(k))
+        sums[k, core] = sums[k, core] + core_in[k]
+        start(first_copies(k, parity))
+
+    def after_first(k, parity):
+        arrive(first_copies(k, parity))
+        if parity == 0:
+            for h in range(n_high):
+                sums[k, core, h, low] = sums[k, core, h, low] + low_first[k // 2, h]
+        else:
+            total = sums[k, core, high]
+            for d in range(1, n_high):
+                total = total + high_first[k // 2, d - 1]
+            sums[k, core, high] = total
+        start(second_copies(k, parity))
+
+    def after_second(k, parity):
+        arrive(second_copies(k, parity))
+        total = sums[k, core, high, low]
+        if parity == 1:
+            total = total + low_second[k // 2]
+        else:
+            for d in range(1, n_high):
+                total = total + high_second[k // 2, d - 1]
+        sums[k, core, high, low] = total
+        start(far_copies(k))
+
+    def load(k):
+        return pltpu.make_async_copy(
+            pattern_hbm.at[:, :, :, pl.ds(k * per_chunk, per_chunk)],
+            pattern_ref.at[k],
+            load_sem.at[k],
+        )
+
+    for k in range(chunks):
+        load(k).start()
+
+    peers = [core_peer, low_peer]
+    peers += [high_peer(d) for d in range(1, n_high)] + [far_peer(d) for d in range(1, n_far)]
+    barrier = pltpu.get_barrier_semaphore()
+    for peer in peers:
+        pl.semaphore_signal(barrier, inc=1, device_id=peer, device_id_type=pl.DeviceIdType.MESH)
     phase_factors(offsets_ref, row_ref, column_ref, cos_ref, sin_ref)
-    bands_theta, _, _, units, band_theta, _ = out_ref.shape
-
-    @pl.loop(0, units)
-    def _(i):
-        def store(band, part, value):
-            out_ref[:, band, part, i] = value.reshape(bands_theta, band_theta, LANES)
-
-        subtree_sum(i, pattern_ref, phi_ref, theta_ref, coarse_ref, cos_ref, sin_ref, store)
+    pl.semaphore_wait(barrier, len(peers))
+
+    def compute(k):
+        load(k).wait()
+
+        @pl.loop(0, per_chunk)
+        def _(unit):
+            def pattern(s, r):
+                return jnp.concatenate(
+                    [pattern_ref[k, s, r, g, unit] for g in range(group)], axis=1
+                )
+
+            def store(band, part, value):
+                value = value.reshape(n_far, 2, band_theta, LANES)
+                for c in range(2):
+                    sums[k, c, band // 2, band % 2, :, part, unit] = value[:, c]
+
+            subtree_sum(pattern, phi_ref, theta_ref, coarse_ref, cos_ref, sin_ref, store)
+
+    stages = ((1, after_core), (FIRST_LAG, after_first), (SECOND_LAG, after_second))
+
+    @pl.loop(0, chunks // 2)
+    def _(pair):
+        for parity in range(2):
+            k = pair * 2 + parity
+            compute(k)
+            start(core_copies(k))
+            for lag, stage in stages[::-1]:
+
+                @pl.when(k >= lag)
+                def _(lag=lag, stage=stage, k=k, parity=parity):
+                    stage(k - lag, (parity - lag) % 2)
+
+    for step in range(chunks, chunks + SECOND_LAG):
+        for lag, stage in stages[::-1]:
+            if step - lag < chunks:
+                stage(step - lag, (step - lag) % 2)
+
+    for k in range(chunks):
+        arrive(far_copies(k))
+        total = sums[k, core, high, low, far]
+        for d in range(1, n_far):
+            total = total + far_in[k, d - 1]
+        out_ref[:, k * per_chunk : (k + 1) * per_chunk] = total
+
+    @pl.loop(0, chunks // 2)
+    def _(pair):
+        for parity in range(2):
+            k = pair * 2 + parity
+            copies = core_copies(k) + first_copies(k, parity) + second_copies(k, parity)
+            for copy in copies + far_copies(k):
+                copy.wait_send()
+
+
+def root_tile(pattern, up_phi_grouped, up_theta, offsets, count_phi, count_theta):
+    held, parts, group, units, polar, azimuth = pattern.shape
+    rows, columns = direction_tables(group, count_phi)
+    band_theta = NT // count_theta
+    n_high, n_far = count_phi // 2, count_theta // 2
+    chunks = min(CHUNKS, units)
+    per_chunk = units // chunks
+    tile = (parts, per_chunk, band_theta, LANES)
+    whole = pl.BlockSpec(memory_space=pltpu.VMEM)
+    peers = max(1, n_high - 1)
+    return pl.pallas_call(
+        root_kernel,
+        out_shape=jax.ShapeDtypeStruct((parts, units, band_theta, LANES), jnp.float32),
+        in_specs=[
+            pl.BlockSpec(memory_space=pl.ANY), whole, whole,
+            pl.BlockSpec(memory_space=pltpu.SMEM), whole, whole,
+        ],
+        out_specs=whole,
+        scratch_shapes=[
+            pltpu.VMEM((chunks, held, parts, group, per_chunk, polar, azimuth), jnp.bfloat16),
+            pltpu.VMEM((held, NT, count_phi * LANES), jnp.float32),
+            pltpu.VMEM((held, NT, count_phi * LANES), jnp.float32),
+            pltpu.VMEM((held * parts * polar, count_phi * LANES), jnp.bfloat16),
+            pltpu.VMEM((chunks, 2, n_high, 2, n_far) + tile, jnp.float32),
+            pltpu.VMEM((chunks, n_high, 2, n_far) + tile, jnp.float32),
+            pltpu.VMEM((chunks // 2, n_high, n_far) + tile, jnp.float32),
+            pltpu.VMEM((chunks // 2, peers, 2, n_far) + tile, jnp.float32),
+            pltpu.VMEM((chunks // 2, peers, n_far) + tile, jnp.float32),
+            pltpu.VMEM((chunks // 2, n_far) + tile, jnp.float32),
+            pltpu.VMEM((chunks, n_far - 1) + tile, jnp.float32),
+            pltpu.SemaphoreType.DMA((chunks,)),
+            pltpu.SemaphoreType.DMA((chunks, 2)),
+            pltpu.SemaphoreType.DMA((chunks, peers, 2)),
+            pltpu.SemaphoreType.DMA((chunks, peers, 2)),
+            pltpu.SemaphoreType.DMA((chunks, n_far - 1, 2)),
+        ],
+        compiler_params=pltpu.CompilerParams(
+            vmem_limit_bytes=60 << 20, collective_id=0, has_side_effects=True
+        ),
+    )(pattern, up_phi_grouped, up_theta, offsets, jnp.asarray(rows), jnp.asarray(columns))
 
 
 def lagrange_matrix(start, frac, width):
@@ -156,24 +364,7 @@
     units = channels // group
     pattern = subtree_pattern.reshape(held, parts, group, units, polar, azimuth)
     up_phi_grouped = grouped_up_phi(up_phi, group, count_phi)
-    rows, columns = direction_tables(group, count_phi)
-    whole = pl.BlockSpec(memory_space=pltpu.VMEM)
-    total = pl.pallas_call(
-        sum_kernel,
-        out_shape=jax.ShapeDtypeStruct(
-            (count_theta, count_phi, parts, units, band_theta, LANES), jnp.float32
-        ),
-        in_specs=[whole, whole, whole, pl.BlockSpec(memory_space=pltpu.SMEM), whole, whole],
-        out_specs=whole,
-        scratch_shapes=[
-            pltpu.VMEM((held, NT, count_phi * LANES), jnp.float32),
-            pltpu.VMEM((held, NT, count_phi * LANES), jnp.float32),
-            pltpu.VMEM((held * parts * polar, count_phi * LANES), jnp.bfloat16),
-        ],
-        compiler_params=pltpu.CompilerParams(vmem_limit_bytes=56 << 20),
-    )(pattern, up_phi_grouped, up_theta, offsets, jnp.asarray(rows), jnp.asarray(columns))
-    partial_band = lax.psum_scatter(total, "theta", scatter_dimension=0, tiled=False)
-    root = lax.psum_scatter(partial_band, "phi", scatter_dimension=0, tiled=False)
+    root = root_tile(pattern, up_phi_grouped, up_theta, offsets, count_phi, count_theta)
     root = root.reshape(parts, units, band_theta, group, band_phi)
     root = root.transpose(0, 3, 1, 2, 4).reshape(parts, channels, band_theta, band_phi)
     padded = padded_2(root, (("theta", 2),), 2, False)

time: 186 us -> 80.7 us (0.43)
  waiting for transfers between devices: 126 us -> 4.7 us
  Pallas kernels: 26.9 us -> 55 us
  between operations: 13.6 us -> 0.23 us
    reduce_scatter x1 -> x0, waiting for transfers between devices: 89.8 us -> none  [per_device(): lax.psum_scatter(total, 'theta', scatter_dimension=0, tiled=False)]
    unnamed x3 -> x0, waiting for transfers between devices: 31 us -> none
    pallas_call x1, Pallas kernels: 26.9 us -> 55 us  [root_tile(): pl.pallas_call(root_kernel, out_shape=jax.ShapeDtypeStruct((parts, units,...]
  transfers between devices with their start and end apart: 6 -> 4, of which waited for: 5 -> 3; matrix products, arithmetic and copies ran while one was open for 0% -> 1% of each run, Pallas kernels for 0% -> 0%
where the time goes in v2:
time: 80.7 us; the launch traced here: 80.4 us
  Pallas kernels  55 us (68%)
  starting transfers between devices  9.43 us (12%)
  local copies, waits for them, and re-layouts  5.69 us (7%)
  waiting for transfers between devices  4.7 us (6%)
  matrix products  3.44 us (4%)
  other arithmetic  1.92 us (2%)
    pallas_call x1, Pallas kernels, root_tile(): pl.pallas_call(root_kernel, out_shape=jax.ShapeDtypeStruct((parts, units,...  55 us
    ppermute x2, starting transfers between devices, padded_2(): lax.ppermute(lax.slice_in_dim(block, block.shape[dim] - width, None, axis...  6.17 us
    ppermute x2, waiting for transfers between devices, padded_2(): lax.ppermute(lax.slice_in_dim(block, 0, width, axis=dim), axis, backward)  3.68 us
    ppermute x2, starting transfers between devices, padded_2(): lax.ppermute(lax.slice_in_dim(block, 0, width, axis=dim), axis, backward)  3.26 us
    unnamed x10, local copies, waits for them, and re-layouts  2.39 us
    dot_general x1, matrix products, per_device(): jnp.einsum('rqop,wp->rqow', field, phi_weights, precision=lax.Precision.H...  1.8 us
    dot_general x1, matrix products, per_device(): jnp.einsum('ot,rqtp->rqop', theta_weights, padded, precision=lax.Precisio...  1.63 us
  transfers between devices with their start and end apart: 4, of which 3 were waited for; matrix products, arithmetic and copies ran while one was open for 1% of the time, Pallas kernels for 0%

profile of v2, /device:TPU:1, one launch (start us, length us, event | category | flops | bytes accessed | tf_op | source)
XLA Modules:
  0.0 80.4 jit_solution(13484277653982230133)
XLA Ops:
  0.0 0.9 %copy.21 = bf16[128,256]{0,1:T(8,128)(2,1)S(1)} copy(bf16[128,256]{1,0:T(8,128)(2,1)} %param.11) | data formatting | bytes 131072 | tf_op args[1]
  1.0 0.1 copy.24
  1.1 0.1 copy.25
  1.2 1.4 %copy.26.theta_ref = bf16[128,64]{1,0:T(8,128)(2,1)} copy(bf16[128,64]{0,1:T(8,128)(2,1)} %param.12) | data formatting | bytes 32768 | tf_op args[2]
  2.7 0.7 pad_maximum_fusion.1.phi_ref
  3.4 55.0 %shard_map.100 = f32[2,16,16,128]{3,2,1,0:T(8,128)} custom-call(bf16[8,2,2,16,64,128]{5,4,3,2,1,0:T(8,128)(2,1)} %bitcast.27, bf16[256,512]{1,0:T(8,128)(2,1)} %pad_maximum_fusion.1.phi_ref, bf16[128,64]{1,0:T(8,128)(2,1)} %copy.26.theta_ref, f32[3,8]{1,0:T(4,128)} %offsets_ref.1, f32[2,128,128]{2,1,0:T(8,128)} %constant.73.clone.row_ref, ...), custom_call_target="tpu_custom_call" | custom-call | tf_op jit(solution)/shard_map/pallas_call | solution.py:308
  58.4 1.3 %reshape.41 = f32[2,16,16,2,64]{4,3,2,1,0:T(2,128)S(1)} reshape(f32[2,16,16,128]{3,2,1,0:T(8,128)} %shard_map.100) | data formatting | bytes 524288 | tf_op jit(solution)/shard_map/reshape | solution.py:368
  59.8 5.1 %collective-permute-start = (f32[2,32,2,64]{3,2,1,0:T(2,128)S(1)}, f32[2,32,2,64]{3,2,1,0:T(2,128)S(1)}, u32[]{:S(2)}, u32[]{:S(2)}) collective-permute-start(f32[2,32,2,64]{3,2,1,0:T(2,128)S(1)} %get-tuple-element.9), channel_id=1, source_target_pairs={{0,1},{1,2},{2,3},{3,4},{4,5},{5,6},{6,7},{8,9},{9,10},{10,11},{11... | collective-permute-start | bytes 98312 | tf_op jit(solution)/shard_map/ppermute | solution.py:26
  64.9 1.9 %collective-permute-start.1 = (f32[2,32,2,64]{3,2,1,0:T(2,128)S(1)}, f32[2,32,2,64]{3,2,1,0:T(2,128)S(1)}, u32[]{:S(2)}, u32[]{:S(2)}) collective-permute-start(f32[2,32,2,64]{3,2,1,0:T(2,128)S(1)} %get-tuple-element.10), channel_id=1, source_target_pairs={{1,0},{2,1},{3,2},{4,3},{5,4},{6,5},{7,6},{9,8},{10,9},{11,10},{12... | collective-permute-start | bytes 98312 | tf_op jit(solution)/shard_map/ppermute | solution.py:29
  67.0 3.5 %collective-permute-done.1 = f32[2,32,2,64]{3,2,1,0:T(2,128)S(1)} collective-permute-done((f32[2,32,2,64]{3,2,1,0:T(2,128)S(1)}, f32[2,32,2,64]{3,2,1,0:T(2,128)S(1)}, u32[]{:S(2)}, u32[]{:S(2)}) %collective-permute-start.1) | collective-permute-done | bytes 32800 | tf_op jit(solution)/shard_map/ppermute | solution.py:29
  70.5 0.1 pad_maximum_fusion
  70.7 0.3 fusion.53
  70.9 0.3 copy.28
  71.3 1.1 %collective-permute-start.2 = (f32[2,32,20,2]{1,3,2,0:T(2,128)S(1)}, f32[2,32,20,2]{1,3,2,0:T(2,128)S(1)}, u32[]{:S(2)}, u32[]{:S(2)}) collective-permute-start(f32[2,32,20,2]{1,3,2,0:T(2,128)S(1)} %copy.28), channel_id=1, source_target_pairs={{0,8},{8,16},{16,24},{24,0},{1,9},{9,17},{17,25},{25,1},{2,10},{10... | collective-permute-start | bytes 30728 | tf_op jit(solution)/shard_map/ppermute | solution.py:26
  72.4 0.3 copy.29
  72.7 1.3 %collective-permute-start.3 = (f32[2,32,20,2]{1,3,2,0:T(2,128)S(1)}, f32[2,32,20,2]{1,3,2,0:T(2,128)S(1)}, u32[]{:S(2)}, u32[]{:S(2)}) collective-permute-start(f32[2,32,20,2]{1,3,2,0:T(2,128)S(1)} %copy.29), channel_id=1, source_target_pairs={{8,0},{16,8},{24,16},{0,24},{9,1},{17,9},{25,17},{1,25},{10,2},{18... | collective-permute-start | bytes 30728 | tf_op jit(solution)/shard_map/ppermute | solution.py:29
  74.0 1.0 %collective-permute-done.2 = f32[2,32,20,2]{1,3,2,0:T(2,128)S(1)} collective-permute-done((f32[2,32,20,2]{1,3,2,0:T(2,128)S(1)}, f32[2,32,20,2]{1,3,2,0:T(2,128)S(1)}, u32[]{:S(2)}, u32[]{:S(2)}) %collective-permute-start.2) | collective-permute-done | bytes 10272 | tf_op jit(solution)/shard_map/ppermute | solution.py:26
  75.0 0.4 copy.30
  75.4 0.1 collective-permute-done.3
  75.6 0.4 copy.31
  75.9 1.6 %convolution_bitcast_fusion = f32[2,32,32,68]{3,2,1,0:T(8,128)S(1)} fusion(f32[2,32,20,2]{3,2,1,0:T(8,128)S(1)} %copy.31, f32[2,32,2,64]{3,2,1,0:T(2,128)S(1)} %collective-permute-done.1, f32[2,32,16,64]{3,2,1,0:T(8,128)S(1)} %bitcast.31, f32[2,32,2,64]{3,2,1,0:T(2,128)S(1)} %collective-permute-done, f32[2,32,20,2]{3,2,1,0:T(8,128)S(1)} %copy.30, ...), kind=kOutput, calls=%fused_computation.1 | convolution fusion | flops 33778560 | bytes 906240 | tf_op jit(solution)/shard_map/ot,rqtp->rqop/dot_general | solution.py:376
  77.6 1.8 %convolution_multiply_fusion = f32[2,32,32,256]{3,2,1,0:T(8,128)S(1)} fusion(f32[2,32,32,68]{3,2,1,0:T(8,128)S(1)} %convolution_bitcast_fusion, f32[256]{0:T(256)S(1)} %get-tuple-element.19, s32[256]{0:T(256)S(1)} %get-tuple-element.16, f32[256]{0:T(256)S(1)} %get-tuple-element.20, s32[256]{0:T(256)S(1)} %get-tuple-element.15, f32[256]{0:T(256)S(1)} %get-tuple-element.18, ...), kind=kOutput, calls=%fused_computation | convolution fusion | flops 428534784 | bytes 2662400 | tf_op jit(solution)/shard_map/rqop,wp->rqow/dot_general | solution.py:377
  79.4 0.2 reduce_sum.9
  79.6 0.8 %broadcast_multiply_fusion = f32[16,32,256]{2,1,0:T(8,128)} fusion(f32[16,32,256]{2,1,0:T(8,128)S(1)} %reduce_sum.9), kind=kLoop, calls=%fused_computation.13 | loop fusion | flops 131072 | bytes 1048576 | tf_op jit(solution)/shard_map/div | solution.py:380
  (17 shorter events, 0.2 us)
Async XLA Ops:
  58.4 8.5 %copy-start.2 = (f32[32]{0:T(128)S(1)}, f32[32]{0:T(128)}, u32[]{:S(2)}) copy-start(f32[32]{0:T(128)} %param.15) | copy-start | bytes 388
  58.4 8.5 %copy-start = (f32[256]{0:T(256)S(1)}, f32[256]{0:T(256)}, u32[]{:S(2)}) copy-start(f32[256]{0:T(256)} %param.17) | copy-start | bytes 3076
  58.4 8.5 %copy-start.1 = (s32[256]{0:T(256)S(1)}, s32[256]{0:T(256)}, u32[]{:S(2)}) copy-start(s32[256]{0:T(256)} %param.16) | copy-start | bytes 3076
  58.4 8.5 %copy-start.3 = (s32[32]{0:T(128)S(1)}, s32[32]{0:T(128)}, u32[]{:S(2)}) copy-start(s32[32]{0:T(128)} %param.14) | copy-start | bytes 388
  59.8 7.1 %collective-permute-start = (f32[2,32,2,64]{3,2,1,0:T(2,128)S(1)}, f32[2,32,2,64]{3,2,1,0:T(2,128)S(1)}, u32[]{:S(2)}, u32[]{:S(2)}) collective-permute-start(f32[2,32,2,64]{3,2,1,0:T(2,128)S(1)} %get-tuple-element.9), channel_id=1, source_target_pairs={{0,1},{1,2},{2,3},{3,4},{4,5},{5,6},{6,7},{8,9},{9,10},{10,11},{11... | collective-permute-start | bytes 98312 | tf_op jit(solution)/shard_map/ppermute | solution.py:26
  64.9 5.6 %collective-permute-start.1 = (f32[2,32,2,64]{3,2,1,0:T(2,128)S(1)}, f32[2,32,2,64]{3,2,1,0:T(2,128)S(1)}, u32[]{:S(2)}, u32[]{:S(2)}) collective-permute-start(f32[2,32,2,64]{3,2,1,0:T(2,128)S(1)} %get-tuple-element.10), channel_id=1, source_target_pairs={{1,0},{2,1},{3,2},{4,3},{5,4},{6,5},{7,6},{9,8},{10,9},{11,10},{12... | collective-permute-start | bytes 98312 | tf_op jit(solution)/shard_map/ppermute | solution.py:29
  71.3 3.8 %collective-permute-start.2 = (f32[2,32,20,2]{1,3,2,0:T(2,128)S(1)}, f32[2,32,20,2]{1,3,2,0:T(2,128)S(1)}, u32[]{:S(2)}, u32[]{:S(2)}) collective-permute-start(f32[2,32,20,2]{1,3,2,0:T(2,128)S(1)} %copy.28), channel_id=1, source_target_pairs={{0,8},{8,16},{16,24},{24,0},{1,9},{9,17},{17,25},{25,1},{2,10},{10... | collective-permute-start | bytes 30728 | tf_op jit(solution)/shard_map/ppermute | solution.py:26
  72.7 2.9 %collective-permute-start.3 = (f32[2,32,20,2]{1,3,2,0:T(2,128)S(1)}, f32[2,32,20,2]{1,3,2,0:T(2,128)S(1)}, u32[]{:S(2)}, u32[]{:S(2)}) collective-permute-start(f32[2,32,20,2]{1,3,2,0:T(2,128)S(1)} %copy.29), channel_id=1, source_target_pairs={{8,0},{16,8},{24,16},{0,24},{9,1},{17,9},{25,17},{1,25},{10,2},{18... | collective-permute-start | bytes 30728 | tf_op jit(solution)/shard_map/ppermute | solution.py:29

commit v3 on v2

--- a/solution.py
+++ b/solution.py
@@ -14,21 +14,6 @@
 CHUNKS = 8
 FIRST_LAG = 3
 SECOND_LAG = 5
-
-
-def padded_2(block, sides, width, periodic):
-    for axis, dim in sides:
-        count = lax.axis_size(axis)
-        forward = [(i, i + 1) for i in range(count - 1)]
-        if periodic:
-            forward.append((count - 1, 0))
-        backward = [(target, source) for source, target in forward]
-        low = lax.ppermute(
-            lax.slice_in_dim(block, block.shape[dim] - width, None, axis=dim), axis, forward
-        )
-        high = lax.ppermute(lax.slice_in_dim(block, 0, width, axis=dim), axis, backward)
-        block = jnp.concatenate([low, block, high], axis=dim)
-    return block
 
 
 def direction_tables(group, bands):
@@ -113,11 +98,38 @@
             store(start // LANES + k, 1, imag_sum[:, piece])
 
 
+def tap_weights(start, frac, node):
+    position = 1.0 + frac
+    weights = [
+        -(position - 1.0) * (position - 2.0) * (position - 3.0) / 6.0,
+        position * (position - 2.0) * (position - 3.0) / 2.0,
+        -position * (position - 1.0) * (position - 3.0) / 2.0,
+        position * (position - 1.0) * (position - 2.0) / 6.0,
+    ]
+    matrix = jnp.zeros(node.shape, jnp.float32)
+    for tap in range(4):
+        matrix = matrix + jnp.where(node == start + tap, weights[tap], 0.0)
+    return matrix
+
+
+def split_dot(a, b):
+    a_high, b_high = a.astype(jnp.bfloat16), b.astype(jnp.bfloat16)
+    a_low = (a - a_high.astype(jnp.float32)).astype(jnp.bfloat16)
+    b_low = (b - b_high.astype(jnp.float32)).astype(jnp.bfloat16)
+
+    def dot(left, right):
+        return jnp.dot(left, right, preferred_element_type=jnp.float32)
+
+    return dot(a_high, b_high) + (dot(a_high, b_low) + dot(a_low, b_high))
+
+
 def root_kernel(
-    pattern_hbm, phi_ref, theta_ref, offsets_ref, row_ref, column_ref, out_ref,
+    pattern_hbm, phi_ref, theta_ref, offsets_ref, row_ref, column_ref,
+    theta_start_ref, theta_frac_ref, phi_start_ref, phi_frac_ref, out_ref,
     pattern_ref, cos_ref, sin_ref, coarse_ref, sums,
     core_in, low_first, high_first, high_second, low_second, far_in,
-    load_sem, core_sem, first_sem, second_sem, far_sem,
+    root, row_low, row_high, edges, edge_left, edge_right, weights_ref,
+    load_sem, core_sem, first_sem, second_sem, far_sem, row_sem, edge_sem,
 ):
     chunks, _, n_high, _, n_far, parts, per_chunk, band_theta, _ = sums.shape
     group = pattern_ref.shape[3]
@@ -189,6 +201,20 @@
             for d in range(1, n_far)
         ]
 
+    count_phi, count_theta = n_high * 2, n_far * 2
+    before = (phi, lax.rem(theta + count_theta - 1, count_theta))
+    after = (phi, lax.rem(theta + 1, count_theta))
+    left = (lax.rem(phi + count_phi - 1, count_phi), theta)
+    right = (lax.rem(phi + 1, count_phi), theta)
+
+    def row_to_after(k):
+        return send(
+            root.at[k, :, :, pl.ds(band_theta - 8, 8)], row_low.at[k], row_sem.at[k, 0], after
+        )
+
+    def row_to_before(k):
+        return send(root.at[k, :, :, pl.ds(0, 8)], row_high.at[k], row_sem.at[k, 1], before)
+
     def start(copies):
         for copy in copies:
             copy.start()
@@ -237,6 +263,7 @@
 
     peers = [core_peer, low_peer]
     peers += [high_peer(d) for d in range(1, n_high)] + [far_peer(d) for d in range(1, n_far)]
+    peers += [before, after, left, right]
     barrier = pltpu.get_barrier_semaphore()
     for peer in peers:
         pl.semaphore_signal(barrier, inc=1, device_id=peer, device_id_type=pl.DeviceIdType.MESH)
@@ -284,7 +311,122 @@
         total = sums[k, core, high, low, far]
         for d in range(1, n_far):
             total = total + far_in[k, d - 1]
-        out_ref[:, k * per_chunk : (k + 1) * per_chunk] = total
+        root[k] = total
+
+        @pl.when(theta < count_theta - 1)
+        def _(k=k):
+            row_to_after(k).start()
+
+        @pl.when(theta > 0)
+        def _(k=k):
+            row_to_before(k).start()
+
+    @pl.when(theta > 0)
+    def _():
+        for k in range(chunks):
+            row_to_after(k).wait_recv()
+
+    @pl.when(theta == 0)
+    def _():
+        row_low[...] = jnp.zeros_like(row_low)
+
+    @pl.when(theta < count_theta - 1)
+    def _():
+        for k in range(chunks):
+            row_to_before(k).wait_recv()
+
+    @pl.when(theta == count_theta - 1)
+    def _():
+        row_high[...] = jnp.zeros_like(row_high)
+
+    units = chunks * per_chunk
+    planes = [(r, k, u) for r in range(parts) for k in range(chunks) for u in range(per_chunk)]
+    stacked = jnp.concatenate(
+        [
+            jnp.concatenate([row_low[k, r, u], root[k, r, u], row_high[k, r, u]], axis=0)
+            for r, k, u in planes
+        ],
+        axis=1,
+    )
+    polar_weights = tap_weights(
+        theta_start_ref[...] - theta * band_theta + 8,
+        theta_frac_ref[...],
+        lax.broadcasted_iota(jnp.int32, (theta_start_ref.shape[0], band_theta + 16), 1),
+    )
+    rows = split_dot(polar_weights, stacked)
+
+    band_phi = LANES // group
+    lane = lax.broadcasted_iota(jnp.int32, (rows.shape[0], LANES), 1)
+    own = 4 * group
+    per_pack = LANES // own
+    plane = [rows[:, j * LANES : (j + 1) * LANES] for j in range(len(planes))]
+    for pack in range(len(planes) // per_pack):
+        packed = jnp.zeros_like(plane[0])
+        for j in range(per_pack):
+            for g in range(group):
+                at = own * j + 4 * g
+                shift = (at - (g * band_phi - 2)) % LANES
+                value = plane[pack * per_pack + j]
+                value = pltpu.roll(value, shift, 1) if shift else value
+                packed = jnp.where((lane >= at) & (lane < at + 4), value, packed)
+        edges[pack] = packed
+    to_right = send(edges, edge_left, edge_sem.at[0], right)
+    to_left = send(edges, edge_right, edge_sem.at[1], left)
+    to_right.start()
+    to_left.start()
+
+    width = phi_start_ref.shape[1]
+    local_start = phi_start_ref[...] - phi * band_phi
+    row = lax.broadcasted_iota(jnp.int32, (LANES, width), 0)
+    own_group, own_node = row // band_phi, lax.rem(row, band_phi)
+    slot = lax.rem(row, own) // 4
+    offset = lax.rem(row, 4)
+    from_left = (row < own) & (offset < 2)
+    from_right = (row >= own) & (row < 2 * own) & (offset >= 2)
+    edge_group = jnp.where(from_left, lax.rem(slot + group - 1, group), slot)
+    edge_node = jnp.where(from_left, offset - 2, band_phi + offset - 2)
+    own_taps = tap_weights(local_start, phi_frac_ref[...], own_node)
+    edge_taps = tap_weights(local_start, phi_frac_ref[...], edge_node)
+    edge_taps = jnp.where(from_left | from_right, edge_taps, 0.0)
+    for g in range(group):
+        columns = slice(g * width, (g + 1) * width)
+        weights_ref[:LANES, columns] = jnp.where(own_group == g, own_taps, 0.0)
+        weights_ref[LANES:, columns] = jnp.where(edge_group == g, edge_taps, 0.0)
+
+    to_right.wait_recv()
+    to_left.wait_recv()
+    operand = []
+    for j in range(len(planes)):
+        pack, place = j // per_pack, j % per_pack
+        from_l, from_r = edge_left[pack], edge_right[pack]
+        shift_l, shift_r = (-own * place) % LANES, (own - own * place) % LANES
+        from_l = pltpu.roll(from_l, shift_l, 1) if shift_l else from_l
+        from_r = pltpu.roll(from_r, shift_r, 1) if shift_r else from_r
+        operand.append(jnp.concatenate([plane[j], jnp.where(lane < own, from_l, from_r)], axis=1))
+    field = split_dot(jnp.concatenate(operand, axis=0), weights_ref[...])
+    incidences = out_ref.shape[0]
+    height = rows.shape[0]
+    power = [None] * incidences
+    for j in range(len(planes)):
+        for g in range(group):
+            value = field[j * height : (j + 1) * height, g * width : (g + 1) * width]
+            at = (g * units + j % units) % incidences
+            power[at] = value * value if power[at] is None else power[at] + value * value
+    for at in range(incidences):
+        out_ref[at] = power[at]
+
+    to_right.wait_send()
+    to_left.wait_send()
+
+    @pl.when(theta < count_theta - 1)
+    def _():
+        for k in range(chunks):
+            row_to_after(k).wait_send()
+
+    @pl.when(theta > 0)
+    def _():
+        for k in range(chunks):
+            row_to_before(k).wait_send()
 
     @pl.loop(0, chunks // 2)
     def _(pair):
@@ -295,7 +437,9 @@
                 copy.wait_send()
 
 
-def root_tile(pattern, up_phi_grouped, up_theta, offsets, count_phi, count_theta):
+def power_sum(
+    pattern, up_phi_grouped, up_theta, offsets, rows_out, columns_out, count_phi, count_theta
+):
     held, parts, group, units, polar, azimuth = pattern.shape
     rows, columns = direction_tables(group, count_phi)
     band_theta = NT // count_theta
@@ -305,12 +449,15 @@
     tile = (parts, per_chunk, band_theta, LANES)
     whole = pl.BlockSpec(memory_space=pltpu.VMEM)
     peers = max(1, n_high - 1)
+    height, width = rows_out[0].shape[0], columns_out[0].shape[0]
+    channels = group * units
+    packs = parts * channels * 4 // LANES
     return pl.pallas_call(
         root_kernel,
-        out_shape=jax.ShapeDtypeStruct((parts, units, band_theta, LANES), jnp.float32),
+        out_shape=jax.ShapeDtypeStruct((channels // 2, height, width), jnp.float32),
         in_specs=[
             pl.BlockSpec(memory_space=pl.ANY), whole, whole,
-            pl.BlockSpec(memory_space=pltpu.SMEM), whole, whole,
+            pl.BlockSpec(memory_space=pltpu.SMEM), whole, whole, whole, whole, whole, whole,
         ],
         out_specs=whole,
         scratch_shapes=[
@@ -325,31 +472,28 @@
             pltpu.VMEM((chunks // 2, peers, n_far) + tile, jnp.float32),
             pltpu.VMEM((chunks // 2, n_far) + tile, jnp.float32),
             pltpu.VMEM((chunks, n_far - 1) + tile, jnp.float32),
+            pltpu.VMEM((chunks,) + tile, jnp.float32),
+            pltpu.VMEM((chunks, parts, per_chunk, 8, LANES), jnp.float32),
+            pltpu.VMEM((chunks, parts, per_chunk, 8, LANES), jnp.float32),
+            pltpu.VMEM((packs, height, LANES), jnp.float32),
+            pltpu.VMEM((packs, height, LANES), jnp.float32),
+            pltpu.VMEM((packs, height, LANES), jnp.float32),
+            pltpu.VMEM((2 * LANES, group * width), jnp.float32),
             pltpu.SemaphoreType.DMA((chunks,)),
             pltpu.SemaphoreType.DMA((chunks, 2)),
             pltpu.SemaphoreType.DMA((chunks, peers, 2)),
             pltpu.SemaphoreType.DMA((chunks, peers, 2)),
             pltpu.SemaphoreType.DMA((chunks, n_far - 1, 2)),
+            pltpu.SemaphoreType.DMA((chunks, 2, 2)),
+            pltpu.SemaphoreType.DMA((2, 2)),
         ],
         compiler_params=pltpu.CompilerParams(
             vmem_limit_bytes=60 << 20, collective_id=0, has_side_effects=True
         ),
-    )(pattern, up_phi_grouped, up_theta, offsets, jnp.asarray(rows), jnp.asarray(columns))
-
-
-def lagrange_matrix(start, frac, width):
-    position = 1.0 + frac
-    weights = [
-        -(position - 1.0) * (position - 2.0) * (position - 3.0) / 6.0,
-        position * (position - 2.0) * (position - 3.0) / 2.0,
-        -position * (position - 1.0) * (position - 3.0) / 2.0,
-        position * (position - 1.0) * (position - 2.0) / 6.0,
-    ]
-    columns = jnp.arange(width, dtype=jnp.int32)[None, :]
-    matrix = jnp.zeros((start.shape[0], width), jnp.float32)
-    for tap in range(4):
-        matrix = matrix + jnp.where(columns == (start + tap)[:, None], weights[tap][:, None], 0.0)
-    return matrix
+    )(
+        pattern, up_phi_grouped, up_theta, offsets, jnp.asarray(rows), jnp.asarray(columns),
+        *(value[:, None] for value in rows_out), *(value[None, :] for value in columns_out),
+    )
 
 
 def per_device(
@@ -357,27 +501,16 @@
 ):
     count_phi = lax.axis_size("phi")
     count_theta = lax.axis_size("theta")
-    band_theta = NT // count_theta
-    band_phi = NP // count_phi
-    group = LANES // band_phi
+    group = LANES * count_phi // NP
     held, parts, channels, polar, azimuth = subtree_pattern.shape
     units = channels // group
     pattern = subtree_pattern.reshape(held, parts, group, units, polar, azimuth)
     up_phi_grouped = grouped_up_phi(up_phi, group, count_phi)
-    root = root_tile(pattern, up_phi_grouped, up_theta, offsets, count_phi, count_theta)
-    root = root.reshape(parts, units, band_theta, group, band_phi)
-    root = root.transpose(0, 3, 1, 2, 4).reshape(parts, channels, band_theta, band_phi)
-    padded = padded_2(root, (("theta", 2),), 2, False)
-    padded = padded_2(padded, (("phi", 3),), 2, True)
-    local_theta = theta_start - lax.axis_index("theta") * band_theta + 2
-    local_phi = phi_start - lax.axis_index("phi") * band_phi + 2
-    theta_weights = lagrange_matrix(local_theta, theta_frac, band_theta + 4)
-    phi_weights = lagrange_matrix(local_phi, phi_frac, band_phi + 4)
-    field = jnp.einsum("ot,rqtp->rqop", theta_weights, padded, precision=lax.Precision.HIGHEST)
-    field = jnp.einsum("rqop,wp->rqow", field, phi_weights, precision=lax.Precision.HIGHEST)
-    subtrees = held * count_phi * count_theta
-    power = (field * field).reshape(4, channels // 2, field.shape[2], field.shape[3])
-    return jnp.sum(power, axis=0) / subtrees
+    power = power_sum(
+        pattern, up_phi_grouped, up_theta, offsets,
+        (theta_start, theta_frac), (phi_start, phi_frac), count_phi, count_theta,
+    )
+    return power / (held * count_phi * count_theta)
 
 
 def solution(mesh):

time: 80.7 us -> 72.8 us (0.902)
  Pallas kernels: 55 us -> 64.6 us
  starting transfers between devices: 9.43 us -> 0 us
  waiting for transfers between devices: 4.7 us -> 0 us
  matrix products: 3.44 us -> 0 us
    pallas_call x1, Pallas kernels: 55 us -> 64.6 us  [power_sum(): pl.pallas_call(root_kernel, out_shape=jax.ShapeDtypeStruct((channels // 2...]
    ppermute x4 -> x0, starting transfers between devices: 9.43 us -> none  [the longest x2 6.17 us: padded_2(): lax.ppermute(lax.slice_in_dim(block, block.shape[dim] - width, None, axis...]
    ppermute x4 -> x0, waiting for transfers between devices: 4.7 us -> none  [the longest x2 3.68 us: padded_2(): lax.ppermute(lax.slice_in_dim(block, 0, width, axis=dim), axis, backward)]
    dot_general x2 -> x0, matrix products: 3.44 us -> none  [the longest x1 1.8 us: per_device(): jnp.einsum('rqop,wp->rqow', field, phi_weights, precision=lax.Precision.H...]
    broadcast_in_dim x0 -> x2, local copies, waits for them, and re-layouts: none -> 2.66 us  [power_sum(): value[:, None]]
    reshape x2 -> x0, local copies, waits for them, and re-layouts: 1.32 us -> none  [per_device(): root = root.reshape(parts, units, band_theta, group, band_phi)]
    div x3 -> x1, other arithmetic: 0.86 us -> 1.88 us  [per_device(): return power / (held * count_phi * count_theta)]
    slice x4 -> x0, local copies, waits for them, and re-layouts: 0.98 us -> none  [the longest x3 0.65 us: padded_2(): lax.slice_in_dim(block, block.shape[dim] - width, None, axis=dim)]
  transfers between devices with their start and end apart: 4 -> 0, of which waited for: 3 -> 0; matrix products, arithmetic and copies ran while one was open for 1% -> 0% of each run, Pallas kernels for 0% -> 0%
where the time goes in v3:
time: 72.8 us; the launch traced here: 72.6 us
  Pallas kernels  64.6 us (89%)
  local copies, waits for them, and re-layouts  5.31 us (7%)
  other arithmetic  2.6 us (4%)
    pallas_call x1, Pallas kernels, power_sum(): pl.pallas_call(root_kernel, out_shape=jax.ShapeDtypeStruct((channels // 2...  64.6 us
    broadcast_in_dim x2, local copies, waits for them, and re-layouts, power_sum(): value[:, None]  2.66 us
    unnamed x2, local copies, waits for them, and re-layouts  2.38 us
    div x1, other arithmetic, per_device(): return power / (held * count_phi * count_theta)  1.88 us

profile of v3, /device:TPU:1, one launch (start us, length us, event | category | flops | bytes accessed | tf_op | source)
XLA Modules:
  0.0 72.6 jit_solution(15729162601624571726)
XLA Ops:
  0.0 1.3 %copy.22.theta_start_ref = s32[32,1]{1,0:T(8,128)} copy(s32[32,1]{0,1:T(1,128)} %bitcast.18) | data formatting | bytes 256 | tf_op jit(solution)/shard_map/broadcast_in_dim | solution.py:495
  1.3 1.3 %copy.23.theta_frac_ref = f32[32,1]{1,0:T(8,128)} copy(f32[32,1]{0,1:T(1,128)} %bitcast.19) | data formatting | bytes 256 | tf_op jit(solution)/shard_map/broadcast_in_dim | solution.py:495
  2.7 1.4 %copy.21.theta_ref = bf16[128,64]{1,0:T(8,128)(2,1)} copy(bf16[128,64]{0,1:T(8,128)(2,1)} %param.12) | data formatting | bytes 32768 | tf_op args[2]
  4.1 0.9 %copy.16 = bf16[128,256]{0,1:T(8,128)(2,1)S(1)} copy(bf16[128,256]{1,0:T(8,128)(2,1)} %param.11) | data formatting | bytes 131072 | tf_op args[1]
  5.1 0.1 copy.19
  5.2 0.1 copy.20
  5.3 0.7 pad_maximum_fusion.phi_ref
  6.1 64.6 %shard_map.100 = f32[16,32,256]{2,1,0:T(8,128)} custom-call(bf16[8,2,2,16,64,128]{5,4,3,2,1,0:T(8,128)(2,1)} %bitcast.12, bf16[256,512]{1,0:T(8,128)(2,1)} %pad_maximum_fusion.phi_ref, bf16[128,64]{1,0:T(8,128)(2,1)} %copy.21.theta_ref, f32[3,8]{1,0:T(4,128)} %offsets_ref.1, f32[2,128,128]{2,1,0:T(8,128)} %constant.10.clone.row_ref, ...), custom_call_target="tpu_custom_call" | custom-call | tf_op jit(solution)/shard_map/pallas_call | solution.py:455
  70.7 1.9 %broadcast_multiply_fusion = f32[16,32,256]{2,1,0:T(8,128)} fusion(f32[16,32,256]{2,1,0:T(8,128)} %shard_map.100), kind=kLoop, calls=%fused_computation.1 | loop fusion | flops 131072 | bytes 1048576 | tf_op jit(solution)/shard_map/div | solution.py:513
  (1 shorter events, 0.0 us)

commit v4 on v3

--- a/solution.py
+++ b/solution.py
@@ -11,9 +11,9 @@
 NT = 128
 NP = 256
 LANES = 128
-CHUNKS = 8
-FIRST_LAG = 3
-SECOND_LAG = 5
+CHUNKS = 16
+FIRST_LAG = 4
+SECOND_LAG = 8
 
 
 def direction_tables(group, bands):
@@ -27,13 +27,19 @@
     return rows.astype(np.float32), columns.astype(np.float32)
 
 
-def grouped_up_phi(up_phi, group, bands):
-    split = up_phi.reshape(up_phi.shape[0], bands, 1, NP // bands)
-    blocks = []
-    for g in range(group):
-        pads = [(0, 0), (0, 0), (g, group - 1 - g), (0, 0)]
-        blocks.append(jnp.pad(split, pads).reshape(up_phi.shape[0], -1))
-    return jnp.concatenate(blocks, axis=0)
+def group_up_phi(source_ref, target_ref, group, bands):
+    depth, band = source_ref.shape[0], NP // bands
+    lane = lax.broadcasted_iota(jnp.int32, (depth, LANES), 1)
+    for a in range(bands):
+        tile, inside = divmod(a * band, LANES)
+        columns = source_ref[:, tile * LANES : (tile + 1) * LANES].astype(jnp.float32)
+        for g in range(group):
+            shift = (g * band - inside) % LANES
+            value = pltpu.roll(columns, shift, 1) if shift else columns
+            value = jnp.where((lane >= g * band) & (lane < (g + 1) * band), value, 0.0)
+            target_ref[g * depth : (g + 1) * depth, a * LANES : (a + 1) * LANES] = value.astype(
+                jnp.bfloat16
+            )
 
 
 def turn_series():
@@ -112,21 +118,22 @@
     return matrix
 
 
-def split_dot(a, b):
+def split_dot(a, b, a_depth=1):
     a_high, b_high = a.astype(jnp.bfloat16), b.astype(jnp.bfloat16)
     a_low = (a - a_high.astype(jnp.float32)).astype(jnp.bfloat16)
     b_low = (b - b_high.astype(jnp.float32)).astype(jnp.bfloat16)
 
     def dot(left, right):
-        return jnp.dot(left, right, preferred_element_type=jnp.float32)
+        numbers = (((a_depth,), (0,)), ((), ()))
+        return lax.dot_general(left, right, numbers, preferred_element_type=jnp.float32)
 
     return dot(a_high, b_high) + (dot(a_high, b_low) + dot(a_low, b_high))
 
 
 def root_kernel(
-    pattern_hbm, phi_ref, theta_ref, offsets_ref, row_ref, column_ref,
+    pattern_hbm, up_phi_ref, up_theta_ref, offsets_ref, row_ref, column_ref,
     theta_start_ref, theta_frac_ref, phi_start_ref, phi_frac_ref, out_ref,
-    pattern_ref, cos_ref, sin_ref, coarse_ref, sums,
+    pattern_ref, phi_ref, theta_ref, cos_ref, sin_ref, coarse_ref, sums,
     core_in, low_first, high_first, high_second, low_second, far_in,
     root, row_low, row_high, edges, edge_left, edge_right, weights_ref,
     load_sem, core_sem, first_sem, second_sem, far_sem, row_sem, edge_sem,
@@ -267,6 +274,8 @@
     barrier = pltpu.get_barrier_semaphore()
     for peer in peers:
         pl.semaphore_signal(barrier, inc=1, device_id=peer, device_id_type=pl.DeviceIdType.MESH)
+    group_up_phi(up_phi_ref, phi_ref, group, n_high * 2)
+    theta_ref[...] = up_theta_ref[...].astype(jnp.float32).T.astype(jnp.bfloat16)
     phase_factors(offsets_ref, row_ref, column_ref, cos_ref, sin_ref)
     pl.semaphore_wait(barrier, len(peers))
 
@@ -295,14 +304,14 @@
             k = pair * 2 + parity
             compute(k)
             start(core_copies(k))
-            for lag, stage in stages[::-1]:
+            for lag, stage in stages:
 
                 @pl.when(k >= lag)
                 def _(lag=lag, stage=stage, k=k, parity=parity):
                     stage(k - lag, (parity - lag) % 2)
 
     for step in range(chunks, chunks + SECOND_LAG):
-        for lag, stage in stages[::-1]:
+        for lag, stage in stages:
             if step - lag < chunks:
                 stage(step - lag, (step - lag) % 2)
 
@@ -351,9 +360,9 @@
     polar_weights = tap_weights(
         theta_start_ref[...] - theta * band_theta + 8,
         theta_frac_ref[...],
-        lax.broadcasted_iota(jnp.int32, (theta_start_ref.shape[0], band_theta + 16), 1),
+        lax.broadcasted_iota(jnp.int32, (band_theta + 16, theta_start_ref.shape[1]), 0),
     )
-    rows = split_dot(polar_weights, stacked)
+    rows = split_dot(polar_weights, stacked, 0)
 
     band_phi = LANES // group
     lane = lax.broadcasted_iota(jnp.int32, (rows.shape[0], LANES), 1)
@@ -438,7 +447,7 @@
 
 
 def power_sum(
-    pattern, up_phi_grouped, up_theta, offsets, rows_out, columns_out, count_phi, count_theta
+    pattern, up_phi, up_theta, offsets, rows_out, columns_out, count_phi, count_theta
 ):
     held, parts, group, units, polar, azimuth = pattern.shape
     rows, columns = direction_tables(group, count_phi)
@@ -462,6 +471,8 @@
         out_specs=whole,
         scratch_shapes=[
             pltpu.VMEM((chunks, held, parts, group, per_chunk, polar, azimuth), jnp.bfloat16),
+            pltpu.VMEM((group * azimuth, count_phi * LANES), jnp.bfloat16),
+            pltpu.VMEM((NT, polar), jnp.bfloat16),
             pltpu.VMEM((held, NT, count_phi * LANES), jnp.float32),
             pltpu.VMEM((held, NT, count_phi * LANES), jnp.float32),
             pltpu.VMEM((held * parts * polar, count_phi * LANES), jnp.bfloat16),
@@ -491,8 +502,8 @@
             vmem_limit_bytes=60 << 20, collective_id=0, has_side_effects=True
         ),
     )(
-        pattern, up_phi_grouped, up_theta, offsets, jnp.asarray(rows), jnp.asarray(columns),
-        *(value[:, None] for value in rows_out), *(value[None, :] for value in columns_out),
+        pattern, up_phi, up_theta.T, offsets, jnp.asarray(rows), jnp.asarray(columns),
+        *(value[None, :] for value in rows_out + columns_out),
     )
 
 
@@ -505,9 +516,8 @@
     held, parts, channels, polar, azimuth = subtree_pattern.shape
     units = channels // group
     pattern = subtree_pattern.reshape(held, parts, group, units, polar, azimuth)
-    up_phi_grouped = grouped_up_phi(up_phi, group, count_phi)
     power = power_sum(
-        pattern, up_phi_grouped, up_theta, offsets,
+        pattern, up_phi, up_theta, offsets,
         (theta_start, theta_frac), (phi_start, phi_frac), count_phi, count_theta,
     )
     return power / (held * count_phi * count_theta)

time: 72.8 us -> 65.4 us (0.90)
  local copies, waits for them, and re-layouts: 5.31 us -> 0 us
  Pallas kernels: 64.6 us -> 63.3 us
    broadcast_in_dim x2 -> x0, local copies, waits for them, and re-layouts: 2.66 us -> none  [power_sum(): value[:, None]]
    unnamed x2 -> x0, local copies, waits for them, and re-layouts: 2.38 us -> none
    pallas_call x1, Pallas kernels: 64.6 us -> 63.3 us  [power_sum(): pl.pallas_call(root_kernel, out_shape=jax.ShapeDtypeStruct((channels // 2...]
where the time goes in v4:
time: 65.4 us; the launch traced here: 65.2 us
  Pallas kernels  63.3 us (97%)
  other arithmetic  1.88 us (3%)
    pallas_call x1, Pallas kernels, power_sum(): pl.pallas_call(root_kernel, out_shape=jax.ShapeDtypeStruct((channels // 2...  63.3 us
    div x1, other arithmetic, per_device(): return power / (held * count_phi * count_theta)  1.88 us

profile of v4, /device:TPU:1, one launch (start us, length us, event | category | flops | bytes accessed | tf_op | source)
XLA Modules:
  0.0 65.2 jit_solution(12404578798376171628)
XLA Ops:
  0.0 63.3 %shard_map.100 = f32[16,32,256]{2,1,0:T(8,128)} custom-call(bf16[8,2,2,16,64,128]{5,4,3,2,1,0:T(8,128)(2,1)} %bitcast.6, bf16[128,256]{1,0:T(8,128)(2,1)} %up_phi_ref.1, bf16[64,128]{1,0:T(8,128)(2,1)} %bitcast.7, f32[3,8]{1,0:T(4,128)} %offsets_ref.1, f32[2,128,128]{2,1,0:T(8,128)} %constant.7.clone.row_ref, f32[2,8,512]{2,1,0:T(8,128)} %constant.8.clone.column_ref, ...), custom_call_target="tpu_custom_call" | custom-call | tf_op jit(solution)/shard_map/pallas_call | solution.py:464
  63.3 1.9 %broadcast_multiply_fusion = f32[16,32,256]{2,1,0:T(8,128)} fusion(f32[16,32,256]{2,1,0:T(8,128)} %shard_map.100), kind=kLoop, calls=%fused_computation | loop fusion | flops 131072 | bytes 1048576 | tf_op jit(solution)/shard_map/div | solution.py:523

commit v5 on v4

--- a/solution.py
+++ b/solution.py
@@ -414,6 +414,7 @@
         operand.append(jnp.concatenate([plane[j], jnp.where(lane < own, from_l, from_r)], axis=1))
     field = split_dot(jnp.concatenate(operand, axis=0), weights_ref[...])
     incidences = out_ref.shape[0]
+    subtrees = cos_ref.shape[0] * count_phi * count_theta
     height = rows.shape[0]
     power = [None] * incidences
     for j in range(len(planes)):
@@ -422,7 +423,7 @@
             at = (g * units + j % units) % incidences
             power[at] = value * value if power[at] is None else power[at] + value * value
     for at in range(incidences):
-        out_ref[at] = power[at]
+        out_ref[at] = power[at] * (1.0 / subtrees)
 
     to_right.wait_send()
     to_left.wait_send()
@@ -516,11 +517,10 @@
     held, parts, channels, polar, azimuth = subtree_pattern.shape
     units = channels // group
     pattern = subtree_pattern.reshape(held, parts, group, units, polar, azimuth)
-    power = power_sum(
+    return power_sum(
         pattern, up_phi, up_theta, offsets,
         (theta_start, theta_frac), (phi_start, phi_frac), count_phi, count_theta,
     )
-    return power / (held * count_phi * count_theta)
 
 
 def solution(mesh):

time: 65.4 us -> 65.4 us (level)
  other arithmetic: 1.88 us -> 0 us
  local copies, waits for them, and re-layouts: 0 us -> 1.88 us
    unnamed x0 -> x1, local copies, waits for them, and re-layouts: none -> 1.88 us
    div x1 -> x0, other arithmetic: 1.88 us -> none  [per_device(): return power / (held * count_phi * count_theta)]
where the time goes in v5:
time: 65.4 us; the launch traced here: 65.2 us
  Pallas kernels  63.3 us (97%)
  local copies, waits for them, and re-layouts  1.88 us (3%)
    pallas_call x1, Pallas kernels, power_sum(): pl.pallas_call(root_kernel, out_shape=jax.ShapeDtypeStruct((channels // 2...  63.3 us
    unnamed x1, local copies, waits for them, and re-layouts  1.88 us

profile of v5, /device:TPU:1, one launch (start us, length us, event | category | flops | bytes accessed | tf_op | source)
XLA Modules:
  0.0 65.2 jit_solution(2334880711921121139)
XLA Ops:
  0.0 63.3 %shard_map.100 = f32[16,32,256]{2,1,0:T(8,128)} custom-call(bf16[8,2,2,16,64,128]{5,4,3,2,1,0:T(8,128)(2,1)} %bitcast.6, bf16[128,256]{1,0:T(8,128)(2,1)} %up_phi_ref.1, bf16[64,128]{1,0:T(8,128)(2,1)} %bitcast.7, f32[3,8]{1,0:T(4,128)} %offsets_ref.1, f32[2,128,128]{2,1,0:T(8,128)} %constant.4.clone.row_ref, f32[2,8,512]{2,1,0:T(8,128)} %constant.5.clone.column_ref, ...), custom_call_target="tpu_custom_call" | custom-call | tf_op jit(solution)/shard_map/pallas_call | solution.py:465
  63.3 1.9 %copy.12 = f32[16,32,256]{2,1,0:T(8,128)} copy(f32[16,32,256]{2,1,0:T(8,128)} %shard_map.100) | data formatting | bytes 1048576
